TPU v7x, 32 devices: a whole 2x2x4 slice. The times are simulated.
32 devices in a mesh: tm: 8 (over z, y), mp: 4 (over x, core).
Axes of the slice: x: 2, y: 2, z: 4, core: 2. Of those that a mesh axis runs over, the one named last changes fastest.
Arguments:
- queries: bfloat16 [1536, 1024], P('tm', 'mp'), may hold values from -8 to 8
- d_queries: bfloat16 [1536, 1024], P('tm', 'mp'), may hold values from -6 to 6
- key_rows: bfloat16 [1536, 1024], P('tm', 'mp'), may hold values from -8 to 8
- value_rows: bfloat16 [1536, 1024], P('tm', 'mp'), may hold values from -6 to 6
- d_key_rows: bfloat16 [1536, 1024], P('tm', 'mp'), may hold values from -6 to 6
- d_value_rows: bfloat16 [1536, 1024], P('tm', 'mp'), may hold values from -6 to 6
- live_flags: int32 [1536], P('tm'), may hold values from 0 to 1, as said below
- out_weight: bfloat16 [1024, 5120], P('mp'), may hold values from -1 to 1
- gate_scale: float32 [5120], P('mp'), may hold values from 0.25 to 1.75
- tokens: bfloat16 [1536, 5120], P('tm', 'mp'), may hold values from -6 to 6
- d_tokens: bfloat16 [1536, 5120], P('tm', 'mp'), may hold values from -6 to 6
Outputs:
- result: bfloat16 [1536, 5120], P('tm', 'mp')
- d_result: bfloat16 [1536, 5120], P('tm', 'mp')
Inputs may be any that keep to these rules, and one draw needn't show every extreme that they name: live_flags are equal within each aligned run of 32 tokens.
All inputs are finite; a program needn't handle non-finite values.
Results may differ from a plain program's by a relative error of at most 0.019.
Values may be sent and summed in bfloat16 or wider, within the bound.
A program may use at most 128 MiB of HBM per device.

v0:
```python
import functools
import math

import jax
import jax.numpy as jnp
from jax import lax
from jax.experimental import pallas as pl
from jax.experimental.pallas import tpu as pltpu
from jax.sharding import PartitionSpec as P

HD = 128
FRAME = 32
MESH = pl.DeviceIdType.MESH
F32 = jnp.float32
BF16 = jnp.bfloat16


def ring_place(t, n):
    return jnp.where(t % 2 == 0, t // 2, n - 1 - t // 2)


def ring_member(r, n):
    return jnp.where(r < n // 2, 2 * r, 2 * (n - 1 - r) + 1)


def flipped(me, j):
    other = me
    bit = 1
    while bit <= j:
        if j & bit:
            other = other + bit * (1 - 2 * ((me // bit) % 2))
        bit *= 2
    return other


def dot_nt(a, b):
    return lax.dot_general(a, b, (((1,), (1,)), ((), ())), preferred_element_type=F32)


def dot_nn(a, b):
    return lax.dot_general(a, b, (((1,), (0,)), ((), ())), preferred_element_type=F32)


def fused(
    n,
    n_mp,
    move_w,
    q_hbm,
    dq_hbm,
    k_hbm,
    v_hbm,
    dk_hbm,
    dv_hbm,
    flags_hbm,
    w_hbm,
    gate_hbm,
    x_hbm,
    dx_hbm,
    out,
    d_out,
    own,
    qcat,
    tkv,
    kv,
    opp,
    m_s,
    l_s,
    c_s,
    a_s,
    g_s,
    ao,
    wbuf,
    acc,
    xbuf,
    flags,
    gate,
    own_sem,
    x_sem,
    small_sem,
    w_local,
    ks,
    kr,
    ws,
    wr,
    as_,
    ar,
):
    rows, width = q_hbm.shape
    heads = width // HD
    cols = out.shape[1]
    half = n // 2
    t = lax.axis_index("tm")
    m = lax.axis_index("mp")
    place = ring_place(t, n)
    right = ring_member((place + 1) % n, n)
    left = ring_member((place + n - 1) % n, n)
    peers = [flipped(m, j) for j in range(n_mp)]
    factor = 1.0 / math.sqrt(HD)

    def lanes(h):
        return slice(h * HD, (h + 1) * HD)

    loads = [
        pltpu.make_async_copy(src, own.at[i], own_sem.at[i])
        for i, src in enumerate((k_hbm, v_hbm, dk_hbm, dv_hbm, q_hbm, dq_hbm))
    ]
    loads.append(pltpu.make_async_copy(flags_hbm, flags, small_sem.at[0]))
    for load in loads:
        load.start()

    barrier = pltpu.get_barrier_semaphore()
    for dev in [(right, m), (left, m)] + [(t, peers[j]) for j in range(1, n_mp)]:
        pl.semaphore_signal(barrier, inc=1, device_id=dev, device_id_type=MESH)
    pl.semaphore_wait(barrier, 1 + n_mp)

    def exists(d, s, p):
        return s < half or (s == half and (p < 2) == (d == 0))

    def kv_copy(h, d, s, p):
        side = slice(d * rows, (d + 1) * rows)
        if s > 1:
            src = kv.at[h, s - 2, p, side]
        elif p < 2:
            src = (k_hbm, v_hbm)[p].at[:, lanes(h)]
        else:
            src = tkv.at[h, p - 2]
        dst = kv.at[h, s - 1, p, side] if s < half else opp.at[h, p]
        return pltpu.make_async_remote_copy(
            src_ref=src,
            dst_ref=dst,
            send_sem=ks.at[h, d, s - 1, p],
            recv_sem=kr.at[h, d, s - 1, p],
            device_id=((right, left)[d], m),
            device_id_type=MESH,
        )

    def send_own(h, pieces):
        for p in pieces:
            for d in (0, 1):
                kv_copy(h, d, 1, p).start()

    def w_copy(h, j):
        span = pl.ds(pl.multiple_of(peers[j] * cols, HD), cols)
        part = slice(h * HD, (h + 1) * HD)
        if j == 0:
            return pltpu.make_async_copy(
                w_hbm.at[part, span], wbuf.at[0, part], w_local.at[h]
            )
        return pltpu.make_async_remote_copy(
            src_ref=w_hbm.at[part, span],
            dst_ref=wbuf.at[j, part],
            send_sem=ws.at[h, j],
            recv_sem=wr.at[h, j],
            device_id=(t, peers[j]),
            device_id_type=MESH,
        )

    def ao_copy(h, j):
        relay = j % 2 == 1 and j > 1
        return pltpu.make_async_remote_copy(
            src_ref=ao.at[h, j - 1 if relay else 0],
            dst_ref=ao.at[h, j],
            send_sem=as_.at[h, j],
            recv_sem=ar.at[h, j],
            device_id=(t, peers[1] if relay else peers[j]),
            device_id_type=MESH,
        )

    send_own(0, (0, 1))
    if move_w:
        for h in range(heads):
            for j in list(range(2, n_mp)) + [1, 0]:
                w_copy(h, j).start()
    x_loads = [
        pltpu.make_async_copy(src, xbuf.at[i], x_sem.at[i])
        for i, src in enumerate((x_hbm, dx_hbm))
    ]
    x_loads.append(pltpu.make_async_copy(gate_hbm, gate, small_sem.at[1]))
    for load in x_loads:
        load.start()
    for load in loads:
        load.wait()

    live = [
        jnp.where(flags[i * FRAME] > 0, 1.0, 0.0).astype(F32)
        for i in range(rows // FRAME)
    ]

    def masked(value, i):
        scale = jnp.full(value.shape, live[i], F32)
        return (value.astype(F32) * scale).astype(BF16)

    for h in range(heads):
        for i in range(rows // FRAME):
            part = slice(i * FRAME, (i + 1) * FRAME)
            tkv[h, 0, part] = masked(own[2, part, lanes(h)], i)
            tkv[h, 1, part] = masked(own[3, part, lanes(h)], i)
        if h == 0:
            send_own(0, (2, 3))
            for g in range(1, heads):
                send_own(g, (0, 1))
        else:
            send_own(h, (2, 3))
    for h in range(heads):
        for i in range(rows // FRAME):
            part = slice(i * FRAME, (i + 1) * FRAME)
            qcat[h, part, 0:HD] = masked(own[5, part, lanes(h)], i)
        qcat[h, :, HD : 2 * HD] = own[4, :, lanes(h)]

    def attend(h, k, tk, values, first):
        queries = qcat[h, :, HD : 2 * HD]
        scores = dot_nt(queries, k)
        d_scores = dot_nt(qcat[h], jnp.concatenate([k, tk], axis=1)) * factor
        peak = jnp.max(scores, axis=1, keepdims=True)
        if not first:
            peak_old = m_s[h]
            peak = jnp.maximum(peak_old, peak)
            rescale = jnp.exp((peak_old - peak) * factor)
        weights = jnp.exp((scores - peak) * factor)
        product = weights * d_scores
        total = jnp.sum(weights, axis=1, keepdims=True)
        slope = jnp.sum(product, axis=1, keepdims=True)
        weights_b = weights.astype(BF16)
        product_b = product.astype(BF16)
        v, tv = values()
        primal = dot_nn(weights_b, v)
        tangent = dot_nn(product_b, v) + dot_nn(weights_b, tv)
        m_s[h] = peak
        if first:
            l_s[h] = total
            c_s[h] = slope
            a_s[h] = primal
            g_s[h] = tangent
        else:
            l_s[h] = l_s[h] * rescale + total
            c_s[h] = c_s[h] * rescale + slope
            a_s[h] = a_s[h] * rescale + primal
            g_s[h] = g_s[h] * rescale + tangent

    def finish(h):
        inverse = 1.0 / l_s[h]
        outputs = a_s[h] * inverse
        d_outputs = g_s[h] * inverse - (c_s[h] * inverse) * outputs
        ao[h, 0, 0:rows] = outputs.astype(BF16)
        ao[h, 0, rows : 2 * rows] = d_outputs.astype(BF16)
        for j in list(range(2, n_mp, 2)) + [1]:
            ao_copy(h, j).start()

    def relay(h):
        for j in range(2, n_mp, 2):
            ao_copy(h, j).wait_recv()
            ao_copy(h, j + 1).start()

    for h in range(heads):
        attend(
            h, own[0, :, lanes(h)], tkv[h, 0], lambda: (own[1, :, lanes(h)], tkv[h, 1]), True
        )
    for s in range(1, half):
        for h in range(heads):
            for p in range(4):
                for d in (0, 1):
                    kv_copy(h, d, s, p).wait_recv()
                    if exists(d, s + 1, p):
                        kv_copy(h, d, s + 1, p).start()
            attend(
                h,
                kv[h, s - 1, 0],
                kv[h, s - 1, 2],
                lambda: (kv[h, s - 1, 1], kv[h, s - 1, 3]),
                False,
            )
    for h in range(heads):
        def opposite(first_p, second_p):
            kv_copy(h, 0, half, first_p).wait_recv()
            kv_copy(h, 1, half, second_p).wait_recv()
            return opp[h, first_p], opp[h, second_p]

        keys, d_keys = opposite(0, 2)
        attend(h, keys, d_keys, lambda: opposite(1, 3), False)
        finish(h)

    step = 2 * HD if cols % (2 * HD) == 0 else cols
    chunks = [slice(c, c + step) for c in range(0, cols, step)]

    def w_part(h, j, chunk):
        part = slice(h * HD, (h + 1) * HD)
        if move_w:
            return wbuf[j, part, chunk]
        return w_hbm[peers[j], part, chunk]

    def project(slots, chunk):
        attn = jnp.concatenate([ao[h, j] for h, j in slots], axis=1)
        weight = jnp.concatenate([w_part(h, j, chunk) for h, j in slots], axis=0)
        return dot_nn(attn, weight)

    if move_w:
        for h in range(heads):
            w_copy(h, 0).wait()
            for j in range(1, n_mp):
                w_copy(h, j).wait_recv()
    for load in x_loads:
        load.wait()
    last = heads - 1
    for h in range(heads):
        ao_copy(h, 1).wait_recv()
    near = [(h, j) for h in range(heads) for j in (0, 1)]
    for chunk in chunks:
        acc[:, chunk] = project(near, chunk)
    for h in range(last):
        relay(h)
    for h in range(last):
        for j in range(3, n_mp, 2):
            ao_copy(h, j).wait_recv()
    far = [(h, j) for h in range(last) for j in range(2, n_mp)]
    for chunk in chunks:
        acc[:, chunk] += project(far, chunk)
    for h in range(heads):
        for s in range(1, half + 1):
            for p in range(4):
                for d in (0, 1):
                    if exists(d, s, p):
                        kv_copy(h, d, s, p).wait_send()
        if move_w:
            for j in range(1, n_mp):
                w_copy(h, j).wait_send()
    relay(last)
    even = [(last, j) for j in range(2, n_mp, 2)]
    for chunk in chunks:
        acc[:, chunk] += project(even, chunk)
    for j in range(3, n_mp, 2):
        ao_copy(last, j).wait_recv()
    odd = [(last, j) for j in range(3, n_mp, 2)]
    for chunk in chunks:
        part = acc[:, chunk] + project(odd, chunk)
        scale = gate[chunk].reshape(1, step)
        out[:, chunk] = (xbuf[0, :, chunk].astype(F32) + scale * part[0:rows]).astype(BF16)
        for i in range(rows // FRAME):
            piece = slice(i * FRAME, (i + 1) * FRAME)
            base = xbuf[1, piece, chunk].astype(F32)
            base = base * jnp.full(base.shape, live[i], F32)
            delta = part[rows + i * FRAME : rows + (i + 1) * FRAME]
            d_out[piece, chunk] = (base + scale * delta).astype(BF16)

    for h in range(heads):
        for j in range(1, n_mp):
            ao_copy(h, j).wait_send()


def per_device(n, n_mp, q, dq, k, v, dk, dv, flags, w, gate, x, dx):
    rows, width = q.shape
    cols = x.shape[1]
    heads = width // HD
    half = n // 2
    move_w = cols % HD == 0
    if not move_w:
        w = lax.all_to_all(w, "mp", split_axis=1, concat_axis=0, tiled=True)
        w = w.reshape(n_mp, width, cols)
    anywhere = pl.BlockSpec(memory_space=pl.ANY)
    vmem = pl.BlockSpec(memory_space=pltpu.VMEM)
    dma = pltpu.SemaphoreType.DMA
    return pl.pallas_call(
        functools.partial(fused, n, n_mp, move_w),
        out_shape=(pltpu.VMEM(x.shape, BF16), pltpu.VMEM(x.shape, BF16)),
        in_specs=[anywhere] * 6
        + [anywhere, anywhere if move_w else vmem, anywhere]
        + [anywhere] * 2,
        out_specs=(vmem, vmem),
        scratch_shapes=[
            pltpu.VMEM((6, rows, width), BF16),
            pltpu.VMEM((heads, rows, 2 * HD), BF16),
            pltpu.VMEM((heads, 2, rows, HD), BF16),
            pltpu.VMEM((heads, half - 1, 4, 2 * rows, HD), BF16),
            pltpu.VMEM((heads, 4, rows, HD), BF16),
            pltpu.VMEM((heads, rows, 1), F32),
            pltpu.VMEM((heads, rows, 1), F32),
            pltpu.VMEM((heads, rows, 1), F32),
            pltpu.VMEM((heads, rows, HD), F32),
            pltpu.VMEM((heads, rows, HD), F32),
            pltpu.VMEM((heads, n_mp, 2 * rows, HD), BF16),
            pltpu.VMEM((n_mp, width, cols) if move_w else (1, 16, HD), BF16),
            pltpu.VMEM((2 * rows, cols), F32),
            pltpu.VMEM((2, rows, cols), BF16),
            pltpu.SMEM((rows,), jnp.int32),
            pltpu.VMEM((cols,), F32),
            dma((6,)),
            dma((2,)),
            dma((2,)),
            dma((heads,)),
            dma((heads, 2, half, 4)),
            dma((heads, 2, half, 4)),
            dma((heads, n_mp)),
            dma((heads, n_mp)),
            dma((heads, n_mp)),
            dma((heads, n_mp)),
        ],
        compiler_params=pltpu.CompilerParams(
            collective_id=0, has_side_effects=True, vmem_limit_bytes=65000000
        ),
    )(q, dq, k, v, dk, dv, flags, w, gate, x, dx)


def solution(mesh):
    both = P("tm", "mp")
    placed = (both,) * 6 + (P("tm"), P("mp", None), P("mp"), both, both)
    return jax.shard_map(
        functools.partial(per_device, mesh.shape["tm"], mesh.shape["mp"]),
        mesh=mesh,
        in_specs=placed,
        out_specs=(both, both),
        check_vma=False,
    )
```

profile of v0, /device:TPU:0, one launch (start us, length us, event | category | flops | bytes accessed | tf_op | source)
XLA Modules:
  0.0 45.2 jit_solution(11000964568044804535)
XLA Ops:
  0.6 43.0 %shard_map.122 = (bf16[192,1280]{1,0:T(8,128)(2,1)S(1)}, bf16[192,1280]{1,0:T(8,128)(2,1)S(1)}) custom-call(bf16[192,256]{1,0:T(8,128)(2,1)} %q_hbm.1, bf16[192,256]{1,0:T(8,128)(2,1)} %dq_hbm.1, bf16[192,256]{1,0:T(8,128)(2,1)} %k_hbm.1, bf16[192,256]{1,0:T(8,128)(2,1)} %v_hbm.1, bf16[192,256]{1,0:T(8,128)(2,1)} %dk_hbm.1, bf16[192,256]{1,0:T(8,128)(2,1)} %dv_hbm.1, ...), custom_call_target="tpu_custom_call" | custom-call | tf_op jit(solution)/shard_map/pallas_call | solution.py:361
  43.7 0.8 %copy.15 = bf16[192,1280]{1,0:T(8,128)(2,1)} copy(bf16[192,1280]{1,0:T(8,128)(2,1)S(1)} %get-tuple-element.2) | data formatting | bytes 983040
  44.5 0.8 %copy.16 = bf16[192,1280]{1,0:T(8,128)(2,1)} copy(bf16[192,1280]{1,0:T(8,128)(2,1)S(1)} %get-tuple-element.3) | data formatting | bytes 983040
where the time goes:
time: 45.4 us; the launch traced here: 45.2 us
  Pallas kernels  43 us (95%)
  local copies, waits for them, and re-layouts  1.56 us (3%)
  between operations  0.64 us (1%)
    pallas_call x1, Pallas kernels, per_device(): pl.pallas_call(functools.partial(fused, n, n_mp, move_w), out_shape=(pltp...  43 us
    unnamed x2, local copies, waits for them, and re-layouts  1.56 us

commit v1 on v0

--- a/solution.py
+++ b/solution.py
@@ -399,11 +399,561 @@
     )(q, dq, k, v, dk, dv, flags, w, gate, x, dx)
 
 
+def spread(
+    n,
+    n_mp,
+    q_hbm,
+    dq_hbm,
+    k_hbm,
+    v_hbm,
+    dk_hbm,
+    dv_hbm,
+    flags_hbm,
+    w_hbm,
+    gate_hbm,
+    x_hbm,
+    dx_hbm,
+    out,
+    d_out,
+    own,
+    tang,
+    qcat,
+    kv,
+    m_s,
+    l_s,
+    c_s,
+    a_s,
+    g_s,
+    res,
+    ao,
+    wbuf,
+    acc,
+    xbuf,
+    flags,
+    gate,
+    own_sem,
+    x_sem,
+    small_sem,
+    w_local,
+    zs,
+    qr,
+    kr,
+    fs,
+    ys,
+    wts,
+    wtr,
+    wxs,
+    wxr,
+    wys,
+    wyr,
+    wzs,
+    wzr,
+    rs,
+    rr,
+    as_,
+    ar,
+):
+    rows, width = q_hbm.shape
+    heads = width // HD
+    cols = out.shape[1]
+    t = lax.axis_index("tm")
+    m = lax.axis_index("mp")
+    z, y = t // 2, t % 2
+    plane, core = m // 2, m % 2
+    side = z // 2
+    role = jnp.where(side == 0, 1 - z % 2, z % 2)
+    far = (side + core) % 2
+
+    def device(side_, role_, core_):
+        z_ = 2 * side_ + jnp.where(side_ == 0, 1 - role_, role_)
+        return (2 * z_ + y, 2 * plane + core_)
+
+    partners = [device(core, j, side) for j in range(heads)]
+    mine = [jnp.logical_and(far == 0, role == j) for j in range(heads)]
+    twin = (t, 2 * plane + 1 - core)
+    across = (t, 2 * (1 - plane) + core)
+    diagonal = (t, 2 * (1 - plane) + 1 - core)
+    row_peer = (2 * z + 1 - y, m)
+    z_peer = device(side, 1 - role, core)
+    factor = 1.0 / math.sqrt(HD)
+
+    def lanes(h):
+        return slice(h * HD, (h + 1) * HD)
+
+    def both(flag, yes, no):
+        pl.when(flag)(yes)
+        pl.when(jnp.logical_not(flag))(no)
+
+    loads = [
+        pltpu.make_async_copy(src, own.at[i], own_sem.at[i])
+        for i, src in enumerate((dq_hbm, dk_hbm, dv_hbm))
+    ]
+    loads.append(pltpu.make_async_copy(flags_hbm, flags, small_sem.at[0]))
+    for load in loads:
+        load.start()
+
+    barrier = pltpu.get_barrier_semaphore()
+    for dev in (twin, across, diagonal, row_peer, z_peer):
+        pl.semaphore_signal(barrier, inc=1, device_id=dev, device_id_type=MESH)
+
+    @pl.when(far == 1)
+    def _():
+        for dev in partners:
+            pl.semaphore_signal(barrier, inc=1, device_id=dev, device_id_type=MESH)
+
+    pl.semaphore_wait(barrier, 5 + heads * far)
+
+    def z_ends(j, p):
+        src = (
+            q_hbm.at[:, lanes(j)],
+            tang.at[0, j],
+            k_hbm.at[:, lanes(j)],
+            tang.at[1, j],
+            v_hbm.at[:, lanes(j)],
+            tang.at[2, j],
+        )[p]
+        if p == 0:
+            return src, qcat.at[role, :, HD : 2 * HD], qr.at[role, 0]
+        if p == 1:
+            return src, qcat.at[role, :, 0:HD], qr.at[role, 1]
+        return src, kv.at[0, far, p - 2, role], kr.at[0, far, p - 2, role]
+
+    def z_remote(j, p):
+        src, dst, sem = z_ends(j, p)
+        return pltpu.make_async_remote_copy(
+            src_ref=src,
+            dst_ref=dst,
+            send_sem=zs.at[j, p],
+            recv_sem=sem,
+            device_id=partners[j],
+            device_id_type=MESH,
+        )
+
+    def z_start(j, pieces):
+        def local():
+            for p in pieces:
+                src, dst, sem = z_ends(j, p)
+                pltpu.make_async_copy(src, dst, sem).start()
+
+        def remote():
+            for p in pieces:
+                z_remote(j, p).start()
+
+        both(mine[j], local, remote)
+
+    def z_sent():
+        for j in range(heads):
+
+            @pl.when(jnp.logical_not(mine[j]))
+            def _():
+                for p in range(6):
+                    z_remote(j, p).wait_send()
+
+    tile = 16
+    tiles = width // tile
+    y_rows = (tiles * 5 // 16) * tile
+    z_rows = (tiles // 2) * tile - y_rows
+    halves = 2 if cols % (2 * HD) == 0 else 1
+    span = cols // halves
+
+    def y_part(index):
+        return pl.ds(pl.multiple_of(index * y_rows, tile), y_rows)
+
+    def z_part(index):
+        return pl.ds(pl.multiple_of(2 * y_rows + index * z_rows, tile), z_rows)
+
+    def w_cols(owner, first, size):
+        return pl.ds(pl.multiple_of(owner * cols + first, HD), size)
+
+    def w_cross(slot, piece):
+        dev = across if slot == 0 else diagonal
+        if piece < halves:
+            part = y_part(y)
+            first, size = piece * span, span
+        else:
+            part = z_part(role)
+            first, size = 0, cols
+        return pltpu.make_async_remote_copy(
+            src_ref=w_hbm.at[part, w_cols(dev[1], first, size)],
+            dst_ref=wbuf.at[2 + slot, part, pl.ds(first, size)],
+            send_sem=wxs.at[slot, piece],
+            recv_sem=wxr.at[slot, piece],
+            device_id=dev,
+            device_id_type=MESH,
+        )
+
+    def w_row(slot, piece):
+        ref = wbuf.at[2 + slot, y_part(y), pl.ds(piece * span, span)]
+        return pltpu.make_async_remote_copy(
+            src_ref=ref,
+            dst_ref=ref,
+            send_sem=wys.at[slot, piece],
+            recv_sem=wyr.at[slot, piece],
+            device_id=row_peer,
+            device_id_type=MESH,
+        )
+
+    def w_z(slot):
+        ref = wbuf.at[2 + slot, z_part(role)]
+        return pltpu.make_async_remote_copy(
+            src_ref=ref,
+            dst_ref=ref,
+            send_sem=wzs.at[slot],
+            recv_sem=wzr.at[slot],
+            device_id=z_peer,
+            device_id_type=MESH,
+        )
+
+    def w_row_relay(piece):
+        for slot in range(2):
+            w_cross(slot, piece).wait_recv()
+            w_row(slot, piece).start()
+
+    def w_z_relay():
+        for slot in range(2):
+            w_cross(slot, halves).wait_recv()
+            w_z(slot).start()
+
+    w_twin = pltpu.make_async_remote_copy(
+        src_ref=w_hbm.at[:, w_cols(twin[1], 0, cols)],
+        dst_ref=wbuf.at[1],
+        send_sem=wts,
+        recv_sem=wtr,
+        device_id=twin,
+        device_id_type=MESH,
+    )
+    w_own = pltpu.make_async_copy(w_hbm.at[:, w_cols(m, 0, cols)], wbuf.at[0], w_local)
+
+    z_start(0, (0, 2))
+    for piece in range(halves + 1):
+        for slot in range(2):
+            w_cross(slot, piece).start()
+    z_start(0, (4,))
+    for load in loads:
+        load.wait()
+
+    live = [
+        jnp.where(flags[i * FRAME] > 0, 1.0, 0.0).astype(F32)
+        for i in range(rows // FRAME)
+    ]
+
+    def masked(value, i):
+        scale = jnp.full(value.shape, live[i], F32)
+        return (value.astype(F32) * scale).astype(BF16)
+
+    for h in range(heads):
+        for a in range(3):
+            for i in range(rows // FRAME):
+                part = slice(i * FRAME, (i + 1) * FRAME)
+                tang[a, h, part] = masked(own[a, part, lanes(h)], i)
+        if h == 0:
+            z_start(0, (1, 3, 5))
+            z_start(1, (0, 2))
+        else:
+            z_start(1, (1, 3, 4, 5))
+    w_twin.start()
+    w_own.start()
+    x_loads = [
+        pltpu.make_async_copy(src, xbuf.at[i], x_sem.at[i])
+        for i, src in enumerate((x_hbm, dx_hbm))
+    ]
+    x_loads.append(pltpu.make_async_copy(gate_hbm, gate, small_sem.at[1]))
+    for load in x_loads:
+        load.start()
+
+    def kv_wait(yr, rel, p, i):
+        ref = kv.at[yr, rel, p, i]
+        pltpu.make_async_copy(ref, ref, kr.at[yr, rel, p, i]).wait()
+
+    def to_twin(yr, p, i):
+        ref = kv.at[yr, far, p, i]
+        return pltpu.make_async_remote_copy(
+            src_ref=ref,
+            dst_ref=ref,
+            send_sem=fs.at[yr, p, i],
+            recv_sem=kr.at[yr, far, p, i],
+            device_id=twin,
+            device_id_type=MESH,
+        )
+
+    def to_row(p, i):
+        return pltpu.make_async_remote_copy(
+            src_ref=kv.at[0, far, p, i],
+            dst_ref=kv.at[1, far, p, i],
+            send_sem=ys.at[p, i],
+            recv_sem=kr.at[1, far, p, i],
+            device_id=row_peer,
+            device_id_type=MESH,
+        )
+
+    def arrivals(yr, rel):
+        def passing():
+            for p in range(4):
+                for i in range(heads):
+                    kv_wait(yr, rel, p, i)
+                    if yr == 0:
+                        to_row(p, i).start()
+                    to_twin(yr, p, i).start()
+
+        def staying():
+            for p in range(4):
+                for i in range(heads):
+                    kv_wait(yr, rel, p, i)
+
+        both(far == rel, passing, staying)
+
+    def attend(yr, rel, i):
+        first = yr == 0 and rel == 0
+        k = kv[yr, rel, 0].reshape(heads * rows, HD)
+        tk = kv[yr, rel, 1].reshape(heads * rows, HD)
+        v = kv[yr, rel, 2].reshape(heads * rows, HD)
+        tv = kv[yr, rel, 3].reshape(heads * rows, HD)
+        scores = dot_nt(qcat[i, :, HD : 2 * HD], k)
+        d_scores = dot_nt(qcat[i], jnp.concatenate([k, tk], axis=1)) * factor
+        peak = jnp.max(scores, axis=1, keepdims=True)
+        if not first:
+            peak_old = m_s[i]
+            peak = jnp.maximum(peak_old, peak)
+            rescale = jnp.exp((peak_old - peak) * factor)
+        weights = jnp.exp((scores - peak) * factor)
+        product = weights * d_scores
+        total = jnp.sum(weights, axis=1, keepdims=True)
+        slope = jnp.sum(product, axis=1, keepdims=True)
+        weights_b = weights.astype(BF16)
+        product_b = product.astype(BF16)
+        wide = dot_nn(weights_b, jnp.concatenate([v, tv], axis=1))
+        primal = wide[:, 0:HD]
+        tangent = dot_nn(product_b, v) + wide[:, HD : 2 * HD]
+        if not first:
+            total = l_s[i] * rescale + total
+            slope = c_s[i] * rescale + slope
+            primal = a_s[i] * rescale + primal
+            tangent = g_s[i] * rescale + tangent
+        if yr == 1 and rel == 1:
+            inverse = 1.0 / total
+            outputs = primal * inverse
+            d_outputs = tangent * inverse - (slope * inverse) * outputs
+            res[i, 0:rows] = outputs.astype(BF16)
+            res[i, rows : 2 * rows] = d_outputs.astype(BF16)
+        else:
+            m_s[i] = peak
+            l_s[i] = total
+            c_s[i] = slope
+            a_s[i] = primal
+            g_s[i] = tangent
+
+    def res_ends(i):
+        return res.at[i], ao.at[role, 0], rr.at[role]
+
+    def res_remote(i):
+        src, dst, sem = res_ends(i)
+        return pltpu.make_async_remote_copy(
+            src_ref=src,
+            dst_ref=dst,
+            send_sem=rs.at[i],
+            recv_sem=sem,
+            device_id=partners[i],
+            device_id_type=MESH,
+        )
+
+    def res_start(i):
+        both(
+            mine[i],
+            lambda: pltpu.make_async_copy(*res_ends(i)).start(),
+            lambda: res_remote(i).start(),
+        )
+
+    for i in range(heads):
+        for a in range(2):
+            ref = qcat.at[i, :, (1 - a) * HD : (2 - a) * HD]
+            pltpu.make_async_copy(ref, ref, qr.at[i, a]).wait()
+    arrivals(0, 0)
+    for i in range(heads):
+        attend(0, 0, i)
+    w_row_relay(0)
+    arrivals(1, 0)
+    for i in range(heads):
+        attend(1, 0, i)
+
+    def w_rest():
+        for piece in range(1, halves):
+            w_row_relay(piece)
+        w_z_relay()
+
+    pl.when(role == 1)(w_rest)
+    arrivals(0, 1)
+    for i in range(heads):
+        attend(0, 1, i)
+    arrivals(1, 1)
+    z_sent()
+    for i in range(heads):
+        attend(1, 1, i)
+        res_start(i)
+    pl.when(role == 0)(w_rest)
+
+    def ao_copy(h, j):
+        relay = j == 3
+        return pltpu.make_async_remote_copy(
+            src_ref=ao.at[h, 2 if relay else 0],
+            dst_ref=ao.at[h, j],
+            send_sem=as_.at[h, j],
+            recv_sem=ar.at[h, j],
+            device_id=across if j == 2 else twin,
+            device_id_type=MESH,
+        )
+
+    def own_heads(h):
+        pltpu.make_async_copy(ao.at[h, 0], ao.at[h, 0], rr.at[h]).wait()
+        ao_copy(h, 2).start()
+        ao_copy(h, 1).start()
+
+    def cross_heads(h):
+        ao_copy(h, 2).wait_recv()
+        ao_copy(h, 3).start()
+
+    step = 2 * HD if cols % (2 * HD) == 0 else cols
+    chunks = [slice(c, c + step) for c in range(0, cols, step)]
+
+    def project(slots, chunk):
+        attn = jnp.concatenate([ao[h, j] for h, j in slots], axis=1)
+        weight = jnp.concatenate(
+            [wbuf[j, h * HD : (h + 1) * HD, chunk] for h, j in slots], axis=0
+        )
+        return dot_nn(attn, weight)
+
+    own_heads(0)
+    cross_heads(0)
+    w_own.wait()
+    w_twin.wait_recv()
+    for slot in range(2):
+        for piece in range(halves):
+            w_row(slot, piece).wait_recv()
+        w_z(slot).wait_recv()
+    ao_copy(0, 1).wait_recv()
+    for load in x_loads:
+        load.wait()
+    ao_copy(0, 3).wait_recv()
+    for chunk in chunks:
+        acc[:, chunk] = project([(0, j) for j in range(n_mp)], chunk)
+    own_heads(1)
+    ao_copy(1, 1).wait_recv()
+    for chunk in chunks:
+        acc[:, chunk] += project([(1, 0), (1, 1)], chunk)
+    cross_heads(1)
+    ao_copy(1, 3).wait_recv()
+    for chunk in chunks:
+        part = acc[:, chunk] + project([(1, 2), (1, 3)], chunk)
+        scale = gate[chunk].reshape(1, step)
+        out[:, chunk] = (xbuf[0, :, chunk].astype(F32) + scale * part[0:rows]).astype(BF16)
+        for i in range(rows // FRAME):
+            piece = slice(i * FRAME, (i + 1) * FRAME)
+            base = xbuf[1, piece, chunk].astype(F32)
+            base = base * jnp.full(base.shape, live[i], F32)
+            delta = part[rows + i * FRAME : rows + (i + 1) * FRAME]
+            d_out[piece, chunk] = (base + scale * delta).astype(BF16)
+
+    for slot in range(2):
+        for piece in range(halves + 1):
+            w_cross(slot, piece).wait_send()
+        for piece in range(halves):
+            w_row(slot, piece).wait_send()
+        w_z(slot).wait_send()
+    w_twin.wait_send()
+    for p in range(4):
+        for i in range(heads):
+            to_row(p, i).wait_send()
+            for yr in range(2):
+                to_twin(yr, p, i).wait_send()
+    for i in range(heads):
+
+        @pl.when(jnp.logical_not(mine[i]))
+        def _():
+            res_remote(i).wait_send()
+
+        for j in range(1, n_mp):
+            ao_copy(i, j).wait_send()
+
+
+def spread_call(n, n_mp, q, dq, k, v, dk, dv, flags, w, gate, x, dx):
+    rows, width = q.shape
+    cols = x.shape[1]
+    heads = width // HD
+    halves = 2 if cols % (2 * HD) == 0 else 1
+    anywhere = pl.BlockSpec(memory_space=pl.ANY)
+    vmem = pl.BlockSpec(memory_space=pltpu.VMEM)
+    dma = pltpu.SemaphoreType.DMA
+    return pl.pallas_call(
+        functools.partial(spread, n, n_mp),
+        out_shape=(pltpu.VMEM(x.shape, BF16), pltpu.VMEM(x.shape, BF16)),
+        in_specs=[anywhere] * 11,
+        out_specs=(vmem, vmem),
+        scratch_shapes=[
+            pltpu.VMEM((3, rows, width), BF16),
+            pltpu.VMEM((3, heads, rows, HD), BF16),
+            pltpu.VMEM((heads, rows, 2 * HD), BF16),
+            pltpu.VMEM((2, 2, 4, heads, rows, HD), BF16),
+            pltpu.VMEM((heads, rows, 1), F32),
+            pltpu.VMEM((heads, rows, 1), F32),
+            pltpu.VMEM((heads, rows, 1), F32),
+            pltpu.VMEM((heads, rows, HD), F32),
+            pltpu.VMEM((heads, rows, HD), F32),
+            pltpu.VMEM((heads, 2 * rows, HD), BF16),
+            pltpu.VMEM((heads, n_mp, 2 * rows, HD), BF16),
+            pltpu.VMEM((n_mp, width, cols), BF16),
+            pltpu.VMEM((2 * rows, cols), F32),
+            pltpu.VMEM((2, rows, cols), BF16),
+            pltpu.SMEM((rows,), jnp.int32),
+            pltpu.VMEM((cols,), F32),
+            dma((3,)),
+            dma((2,)),
+            dma((2,)),
+            dma,
+            dma((heads, 6)),
+            dma((heads, 2)),
+            dma((2, 2, 4, heads)),
+            dma((2, 4, heads)),
+            dma((4, heads)),
+            dma,
+            dma,
+            dma((2, halves + 1)),
+            dma((2, halves + 1)),
+            dma((2, halves)),
+            dma((2, halves)),
+            dma((2,)),
+            dma((2,)),
+            dma((heads,)),
+            dma((heads,)),
+            dma((heads, n_mp)),
+            dma((heads, n_mp)),
+        ],
+        compiler_params=pltpu.CompilerParams(
+            collective_id=0, has_side_effects=True, vmem_limit_bytes=65000000
+        ),
+    )(q, dq, k, v, dk, dv, flags, w, gate, x, dx)
+
+
+def spreads(n, n_mp, q, x):
+    cores = planes = sides = 2
+    heads = q.shape[1] // HD
+    return (
+        n_mp == planes * cores
+        and heads == 2
+        and n == 2 * sides * heads
+        and x.shape[1] % HD == 0
+        and q.shape[0] % FRAME == 0
+    )
+
+
+def program(n, n_mp, q, dq, k, v, dk, dv, flags, w, gate, x, dx):
+    call = spread_call if spreads(n, n_mp, q, x) else per_device
+    return call(n, n_mp, q, dq, k, v, dk, dv, flags, w, gate, x, dx)
+
+
 def solution(mesh):
     both = P("tm", "mp")
     placed = (both,) * 6 + (P("tm"), P("mp", None), P("mp"), both, both)
     return jax.shard_map(
-        functools.partial(per_device, mesh.shape["tm"], mesh.shape["mp"]),
+        functools.partial(program, mesh.shape["tm"], mesh.shape["mp"]),
         mesh=mesh,
         in_specs=placed,
         out_specs=(both, both),

time: 45.4 us -> 46 us (1.013)
  Pallas kernels: 43 us -> 43.6 us
    pallas_call x1, Pallas kernels: 43 us -> 43.6 us  [spread_call(): pl.pallas_call(functools.partial(spread, n, n_mp), out_shape=(pltpu.VMEM(...]
where the time goes in v1:
time: 46 us; the launch traced here: 45.8 us
  Pallas kernels  43.6 us (95%)
  local copies, waits for them, and re-layouts  1.56 us (3%)
  between operations  0.64 us (1%)
    pallas_call x1, Pallas kernels, spread_call(): pl.pallas_call(functools.partial(spread, n, n_mp), out_shape=(pltpu.VMEM(...  43.6 us
    unnamed x2, local copies, waits for them, and re-layouts  1.56 us

profile of v1, /device:TPU:0, one launch (start us, length us, event | category | flops | bytes accessed | tf_op | source)
XLA Modules:
  0.0 45.8 jit_solution(16962520662859336408)
XLA Ops:
  0.6 43.6 %shard_map.122 = (bf16[192,1280]{1,0:T(8,128)(2,1)S(1)}, bf16[192,1280]{1,0:T(8,128)(2,1)S(1)}) custom-call(bf16[192,256]{1,0:T(8,128)(2,1)} %q_hbm.1, bf16[192,256]{1,0:T(8,128)(2,1)} %dq_hbm.1, bf16[192,256]{1,0:T(8,128)(2,1)} %k_hbm.1, bf16[192,256]{1,0:T(8,128)(2,1)} %v_hbm.1, bf16[192,256]{1,0:T(8,128)(2,1)} %dk_hbm.1, bf16[192,256]{1,0:T(8,128)(2,1)} %dv_hbm.1, ...), custom_call_target="tpu_custom_call" | custom-call | tf_op jit(solution)/shard_map/pallas_call | solution.py:885
  44.3 0.8 %copy.15 = bf16[192,1280]{1,0:T(8,128)(2,1)} copy(bf16[192,1280]{1,0:T(8,128)(2,1)S(1)} %get-tuple-element.2) | data formatting | bytes 983040
  45.0 0.8 %copy.16 = bf16[192,1280]{1,0:T(8,128)(2,1)} copy(bf16[192,1280]{1,0:T(8,128)(2,1)S(1)} %get-tuple-element.3) | data formatting | bytes 983040

commit v2 on v0

--- a/solution.py
+++ b/solution.py
@@ -399,11 +399,546 @@
     )(q, dq, k, v, dk, dv, flags, w, gate, x, dx)
 
 
+def gathered(
+    n,
+    n_mp,
+    subs,
+    q_hbm,
+    dq_hbm,
+    k_hbm,
+    v_hbm,
+    dk_hbm,
+    dv_hbm,
+    flags_hbm,
+    w_hbm,
+    gate_hbm,
+    x_hbm,
+    dx_hbm,
+    out,
+    d_out,
+    own,
+    qpack,
+    pack,
+    qcat,
+    kv,
+    m_s,
+    l_s,
+    c_s,
+    a_s,
+    g_s,
+    res,
+    ao,
+    wbuf,
+    acc,
+    xbuf,
+    flags,
+    gate,
+    own_sem,
+    raw_sem,
+    x_sem,
+    small_sem,
+    w_local,
+    qs_,
+    qr,
+    ks,
+    kr,
+    fs,
+    wts,
+    wtr,
+    wxs,
+    wxr,
+    wys,
+    wyr,
+    rs,
+    rr,
+    as_,
+    ar,
+):
+    rows, width = q_hbm.shape
+    heads = width // HD
+    cols = out.shape[1]
+    part = rows // subs
+    t = lax.axis_index("tm")
+    m = lax.axis_index("mp")
+    z, y = t // 2, t % 2
+    plane, core = m // 2, m % 2
+    side = z // 2
+    role = jnp.where(side == 0, 1 - z % 2, z % 2)
+    far = (side + core) % 2
+    home = role == 0
+    itself = jnp.logical_and(home, jnp.logical_and(side == core, y == core))
+
+    def chip(side_, role_):
+        return 2 * side_ + jnp.where(side_ == 0, 1 - role_, role_)
+
+    homes = [(2 * chip(core, 0) + j, 2 * plane + y) for j in range(heads)]
+    at_home = [jnp.logical_and(itself, y == j) for j in range(heads)]
+    sources = [
+        (2 * chip((side + i // 2) % 2, i % 2) + core, 2 * plane + side)
+        for i in range(4)
+    ]
+    twin = (t, 2 * plane + 1 - core)
+    across = (t, 2 * (1 - plane) + core)
+    diagonal = (t, 2 * (1 - plane) + 1 - core)
+    row_peer = (2 * z + 1 - y, m)
+    factor = 1.0 / math.sqrt(HD)
+
+    def lanes(h):
+        return slice(h * HD, (h + 1) * HD)
+
+    def both(flag, yes, no):
+        pl.when(flag)(yes)
+        pl.when(jnp.logical_not(flag))(no)
+
+    def unless(flag, no):
+        pl.when(jnp.logical_not(flag))(no)
+
+    barrier = pltpu.get_barrier_semaphore()
+
+    def greet(dev):
+        pl.semaphore_signal(barrier, inc=1, device_id=dev, device_id_type=MESH)
+
+    for j in range(heads):
+        unless(at_home[j], lambda: greet(homes[j]))
+
+    @pl.when(home)
+    def _():
+        for i in (3, 2, 1):
+            greet(sources[i])
+        unless(itself, lambda: greet(sources[0]))
+
+    for dev in (across, diagonal, row_peer, twin):
+        greet(dev)
+
+    loads = [
+        pltpu.make_async_copy(src, own.at[i], own_sem.at[i])
+        for i, src in enumerate((dq_hbm, dk_hbm, dv_hbm))
+    ]
+    loads.append(pltpu.make_async_copy(flags_hbm, flags, small_sem.at[0]))
+    raw = []
+    for j in range(heads):
+        for i, (src, dst) in enumerate(
+            (
+                (q_hbm, qpack.at[j, :, HD : 2 * HD]),
+                (k_hbm, pack.at[j, 0]),
+                (v_hbm, pack.at[j, 2]),
+            )
+        ):
+            raw.append(
+                pltpu.make_async_copy(src.at[:, lanes(j)], dst, raw_sem.at[j, i])
+            )
+    for load in loads + raw:
+        load.start()
+    for load in loads:
+        load.wait()
+
+    live = [
+        jnp.where(flags[i * FRAME] > 0, 1.0, 0.0).astype(F32)
+        for i in range(rows // FRAME)
+    ]
+
+    def masked(value, i):
+        scale = jnp.full(value.shape, live[i], F32)
+        return (value.astype(F32) * scale).astype(BF16)
+
+    for h in range(heads):
+        for i in range(rows // FRAME):
+            piece = slice(i * FRAME, (i + 1) * FRAME)
+            qpack[h, piece, 0:HD] = masked(own[0, piece, lanes(h)], i)
+            pack[h, 1, piece] = masked(own[1, piece, lanes(h)], i)
+            pack[h, 3, piece] = masked(own[2, piece, lanes(h)], i)
+    for load in raw:
+        load.wait()
+
+    pl.semaphore_wait(
+        barrier,
+        4 + heads + 4 * home.astype(jnp.int32) - 2 * itself.astype(jnp.int32),
+    )
+
+    def q_ends(j):
+        slot = 2 * far + role
+        return qpack.at[j], qcat.at[slot], qr.at[slot]
+
+    def kv_ends(j, sub):
+        blk = 2 * y + role
+        src = pack.at[j, :, sub * part : (sub + 1) * part]
+        return src, kv.at[far, sub, :, blk], kr.at[far, sub, blk]
+
+    def remote(ends, send_sem, dev):
+        src, dst, sem = ends
+        return pltpu.make_async_remote_copy(
+            src_ref=src,
+            dst_ref=dst,
+            send_sem=send_sem,
+            recv_sem=sem,
+            device_id=dev,
+            device_id_type=MESH,
+        )
+
+    def q_remote(j):
+        return remote(q_ends(j), qs_.at[j], homes[j])
+
+    def kv_remote(j, sub):
+        return remote(kv_ends(j, sub), ks.at[j, sub], homes[j])
+
+    for j in range(heads):
+        both(
+            at_home[j],
+            lambda: pltpu.make_async_copy(*q_ends(j)).start(),
+            lambda: q_remote(j).start(),
+        )
+    for sub in range(subs):
+        for j in range(heads):
+            both(
+                at_home[j],
+                lambda: pltpu.make_async_copy(*kv_ends(j, sub)).start(),
+                lambda: kv_remote(j, sub).start(),
+            )
+
+    tile = 16
+    y_rows = (width // tile * 5 // 16) * tile
+    rest = slice(2 * y_rows, width)
+    halves = 2 if cols % (2 * HD) == 0 else 1
+    span = cols // halves
+
+    def y_part(index):
+        return pl.ds(pl.multiple_of(index * y_rows, tile), y_rows)
+
+    def w_cols(owner, first, size):
+        return pl.ds(pl.multiple_of(owner * cols + first, HD), size)
+
+    def w_cross(slot, piece):
+        dev = across if slot == 0 else diagonal
+        if piece < halves:
+            rows_ = y_part(y)
+            first, size = piece * span, span
+        else:
+            rows_ = rest
+            first, size = (piece - halves) * span, span
+        return remote(
+            (
+                w_hbm.at[rows_, w_cols(dev[1], first, size)],
+                wbuf.at[2 + slot, rows_, pl.ds(first, size)],
+                wxr.at[slot, piece],
+            ),
+            wxs.at[slot, piece],
+            dev,
+        )
+
+    def w_row(slot, piece):
+        ref = wbuf.at[2 + slot, y_part(y), pl.ds(piece * span, span)]
+        return remote((ref, ref, wyr.at[slot, piece]), wys.at[slot, piece], row_peer)
+
+    def w_row_relay(piece):
+        for slot in range(2):
+            w_cross(slot, piece).wait_recv()
+            w_row(slot, piece).start()
+
+    w_twin = remote(
+        (w_hbm.at[:, w_cols(twin[1], 0, cols)], wbuf.at[1], wtr), wts, twin
+    )
+    w_own = pltpu.make_async_copy(w_hbm.at[:, w_cols(m, 0, cols)], wbuf.at[0], w_local)
+
+    for piece in range(2 * halves):
+        for slot in range(2):
+            w_cross(slot, piece).start()
+    w_twin.start()
+    w_own.start()
+    x_loads = [
+        pltpu.make_async_copy(src, xbuf.at[i], x_sem.at[i])
+        for i, src in enumerate((x_hbm, dx_hbm))
+    ]
+    x_loads.append(pltpu.make_async_copy(gate_hbm, gate, small_sem.at[1]))
+    for load in x_loads:
+        load.start()
+
+    def to_twin(rel, sub, i):
+        blk = 2 * core + i
+        ref = kv.at[rel, sub, :, blk]
+        return remote((ref, ref, kr.at[rel, sub, blk]), fs.at[rel, sub, i], twin)
+
+    def kv_wait(rel, sub, blk):
+        ref = kv.at[rel, sub, :, blk]
+        pltpu.make_async_copy(ref, ref, kr.at[rel, sub, blk]).wait()
+
+    def arrivals(rel, sub):
+        for i in range(2):
+            kv_wait(rel, sub, 2 * core + i)
+            to_twin(rel, sub, i).start()
+        for i in range(2):
+            kv_wait(rel, sub, 2 * (1 - core) + i)
+
+    def q_wait(i):
+        pltpu.make_async_copy(qcat.at[i], qcat.at[i], qr.at[i]).wait()
+
+    def attend(rel, sub, i):
+        first = rel == 0 and sub == 0
+        keys = 4 * part
+        k, tk, v, tv = (kv[rel, sub, p].reshape(keys, HD) for p in range(4))
+        scores = dot_nt(qcat[i, :, HD : 2 * HD], k)
+        d_scores = dot_nt(qcat[i], jnp.concatenate([k, tk], axis=1)) * factor
+        peak = jnp.max(scores, axis=1, keepdims=True)
+        if not first:
+            peak_old = m_s[i]
+            peak = jnp.maximum(peak_old, peak)
+            rescale = jnp.exp((peak_old - peak) * factor)
+        weights = jnp.exp((scores - peak) * factor)
+        product = weights * d_scores
+        total = jnp.sum(weights, axis=1, keepdims=True)
+        slope = jnp.sum(product, axis=1, keepdims=True)
+        weights_b = weights.astype(BF16)
+        product_b = product.astype(BF16)
+        wide = dot_nn(weights_b, jnp.concatenate([v, tv], axis=1))
+        primal = wide[:, 0:HD]
+        tangent = dot_nn(product_b, v) + wide[:, HD : 2 * HD]
+        if not first:
+            total = l_s[i] * rescale + total
+            slope = c_s[i] * rescale + slope
+            primal = a_s[i] * rescale + primal
+            tangent = g_s[i] * rescale + tangent
+        if rel == 1 and sub == subs - 1:
+            inverse = 1.0 / total
+            outputs = primal * inverse
+            d_outputs = tangent * inverse - (slope * inverse) * outputs
+            res[i, 0] = outputs.astype(BF16)
+            res[i, 1] = d_outputs.astype(BF16)
+        else:
+            m_s[i] = peak
+            l_s[i] = total
+            c_s[i] = slope
+            a_s[i] = primal
+            g_s[i] = tangent
+
+    def res_ends(i, a):
+        return res.at[i, a], ao.at[y, 0, a], rr.at[y, a]
+
+    def res_remote(i, a):
+        return remote(res_ends(i, a), rs.at[i, a], sources[i])
+
+    def res_start(i):
+        def local():
+            for a in range(2):
+                pltpu.make_async_copy(*res_ends(i, a)).start()
+
+        def away():
+            for a in range(2):
+                res_remote(i, a).start()
+
+        if i == 0:
+            both(itself, local, away)
+        else:
+            away()
+
+    @pl.when(home)
+    def _():
+        q_wait(0)
+        q_wait(1)
+        for sub in range(subs):
+            arrivals(0, sub)
+            for i in (0, 1):
+                attend(0, sub, i)
+        w_row_relay(0)
+        q_wait(2)
+        q_wait(3)
+        for sub in range(subs):
+            for i in (2, 3):
+                attend(0, sub, i)
+        for piece in range(1, halves):
+            w_row_relay(piece)
+        for sub in range(subs):
+            arrivals(1, sub)
+            for i in (2, 3, 0, 1):
+                attend(1, sub, i)
+                if sub == subs - 1:
+                    res_start(i)
+
+    @pl.when(jnp.logical_not(home))
+    def _():
+        for piece in range(halves):
+            w_row_relay(piece)
+
+    def ao_copy(h, j, a):
+        src = ao.at[h, 2 if j == 3 else 0, a]
+        dst = ao.at[h, j, a]
+        dev = across if j == 2 else twin
+        return remote((src, dst, ar.at[h, j, a]), as_.at[h, j, a], dev)
+
+    def own_heads(h, a):
+        ref = ao.at[h, 0, a]
+        pltpu.make_async_copy(ref, ref, rr.at[h, a]).wait()
+        ao_copy(h, 2, a).start()
+        ao_copy(h, 1, a).start()
+
+    def cross_heads(h, a):
+        ao_copy(h, 2, a).wait_recv()
+        ao_copy(h, 3, a).start()
+
+    step = 2 * HD if cols % (2 * HD) == 0 else cols
+    chunks = [slice(c, c + step) for c in range(0, cols, step)]
+
+    def project(slots, a, chunk):
+        attn = jnp.concatenate([ao[h, j, a] for h, j in slots], axis=1)
+        weight = jnp.concatenate(
+            [wbuf[j, h * HD : (h + 1) * HD, chunk] for h, j in slots], axis=0
+        )
+        return dot_nn(attn, weight)
+
+    own_plane = [(h, j) for j in (0, 1) for h in range(heads)]
+    other_plane = [(h, j) for j in (2, 3) for h in range(heads)]
+    for a in range(2):
+        for h in range(heads):
+            own_heads(h, a)
+    w_own.wait()
+    w_twin.wait_recv()
+    for load in x_loads:
+        load.wait()
+    for a in range(2):
+        for h in range(heads):
+            ao_copy(h, 1, a).wait_recv()
+        for chunk in chunks:
+            acc[a, :, chunk] = project(own_plane, a, chunk)
+    for slot in range(2):
+        for piece in range(halves, 2 * halves):
+            w_cross(slot, piece).wait_recv()
+        for piece in range(halves):
+            w_row(slot, piece).wait_recv()
+    for a in range(2):
+        for h in range(heads):
+            cross_heads(h, a)
+    for h in range(heads):
+        ao_copy(h, 3, 0).wait_recv()
+    for chunk in chunks:
+        total = acc[0, :, chunk] + project(other_plane, 0, chunk)
+        scale = gate[chunk].reshape(1, step)
+        out[:, chunk] = (xbuf[0, :, chunk].astype(F32) + scale * total).astype(BF16)
+    for h in range(heads):
+        ao_copy(h, 3, 1).wait_recv()
+    for chunk in chunks:
+        total = acc[1, :, chunk] + project(other_plane, 1, chunk)
+        scale = gate[chunk].reshape(1, step)
+        for i in range(rows // FRAME):
+            piece = slice(i * FRAME, (i + 1) * FRAME)
+            base = xbuf[1, piece, chunk].astype(F32)
+            base = base * jnp.full(base.shape, live[i], F32)
+            d_out[piece, chunk] = (base + scale * total[piece]).astype(BF16)
+
+    for j in range(heads):
+
+        def sent():
+            q_remote(j).wait_send()
+            for sub in range(subs):
+                kv_remote(j, sub).wait_send()
+
+        unless(at_home[j], sent)
+    for slot in range(2):
+        for piece in range(2 * halves):
+            w_cross(slot, piece).wait_send()
+        for piece in range(halves):
+            w_row(slot, piece).wait_send()
+    w_twin.wait_send()
+
+    @pl.when(home)
+    def _():
+        for rel in range(2):
+            for sub in range(subs):
+                for i in range(2):
+                    to_twin(rel, sub, i).wait_send()
+        for i in range(1, 4):
+            for a in range(2):
+                res_remote(i, a).wait_send()
+
+        @pl.when(jnp.logical_not(itself))
+        def _():
+            for a in range(2):
+                res_remote(0, a).wait_send()
+
+    for h in range(heads):
+        for j in range(1, n_mp):
+            for a in range(2):
+                ao_copy(h, j, a).wait_send()
+
+
+def gathered_call(n, n_mp, q, dq, k, v, dk, dv, flags, w, gate, x, dx):
+    rows, width = q.shape
+    cols = x.shape[1]
+    heads = width // HD
+    halves = 2 if cols % (2 * HD) == 0 else 1
+    subs = 3 if rows % (3 * FRAME) == 0 else 1
+    part = rows // subs
+    anywhere = pl.BlockSpec(memory_space=pl.ANY)
+    vmem = pl.BlockSpec(memory_space=pltpu.VMEM)
+    dma = pltpu.SemaphoreType.DMA
+    return pl.pallas_call(
+        functools.partial(gathered, n, n_mp, subs),
+        out_shape=(pltpu.VMEM(x.shape, BF16), pltpu.VMEM(x.shape, BF16)),
+        in_specs=[anywhere] * 11,
+        out_specs=(vmem, vmem),
+        scratch_shapes=[
+            pltpu.VMEM((3, rows, width), BF16),
+            pltpu.VMEM((heads, rows, 2 * HD), BF16),
+            pltpu.VMEM((heads, 4, rows, HD), BF16),
+            pltpu.VMEM((4, rows, 2 * HD), BF16),
+            pltpu.VMEM((2, subs, 4, 4, part, HD), BF16),
+            pltpu.VMEM((4, rows, 1), F32),
+            pltpu.VMEM((4, rows, 1), F32),
+            pltpu.VMEM((4, rows, 1), F32),
+            pltpu.VMEM((4, rows, HD), F32),
+            pltpu.VMEM((4, rows, HD), F32),
+            pltpu.VMEM((4, 2, rows, HD), BF16),
+            pltpu.VMEM((heads, n_mp, 2, rows, HD), BF16),
+            pltpu.VMEM((n_mp, width, cols), BF16),
+            pltpu.VMEM((2, rows, cols), F32),
+            pltpu.VMEM((2, rows, cols), BF16),
+            pltpu.SMEM((rows,), jnp.int32),
+            pltpu.VMEM((cols,), F32),
+            dma((3,)),
+            dma((heads, 3)),
+            dma((2,)),
+            dma((2,)),
+            dma,
+            dma((heads,)),
+            dma((4,)),
+            dma((heads, subs)),
+            dma((2, subs, 4)),
+            dma((2, subs, 2)),
+            dma,
+            dma,
+            dma((2, 2 * halves)),
+            dma((2, 2 * halves)),
+            dma((2, halves)),
+            dma((2, halves)),
+            dma((4, 2)),
+            dma((heads, 2)),
+            dma((heads, n_mp, 2)),
+            dma((heads, n_mp, 2)),
+        ],
+        compiler_params=pltpu.CompilerParams(
+            collective_id=0, has_side_effects=True, vmem_limit_bytes=65000000
+        ),
+    )(q, dq, k, v, dk, dv, flags, w, gate, x, dx)
+
+
+def gathers(n, n_mp, q, x):
+    heads = q.shape[1] // HD
+    return (
+        n_mp == 4
+        and n == 8
+        and heads == 2
+        and x.shape[1] % HD == 0
+        and q.shape[0] % FRAME == 0
+    )
+
+
+def program(n, n_mp, q, dq, k, v, dk, dv, flags, w, gate, x, dx):
+    call = gathered_call if gathers(n, n_mp, q, x) else per_device
+    return call(n, n_mp, q, dq, k, v, dk, dv, flags, w, gate, x, dx)
+
+
 def solution(mesh):
     both = P("tm", "mp")
     placed = (both,) * 6 + (P("tm"), P("mp", None), P("mp"), both, both)
     return jax.shard_map(
-        functools.partial(per_device, mesh.shape["tm"], mesh.shape["mp"]),
+        functools.partial(program, mesh.shape["tm"], mesh.shape["mp"]),
         mesh=mesh,
         in_specs=placed,
         out_specs=(both, both),

time: 45.4 us -> 46.5 us (1.024)
  Pallas kernels: 43 us -> 43.9 us
    pallas_call x1, Pallas kernels: 43 us -> 43.9 us  [gathered_call(): pl.pallas_call(functools.partial(gathered, n, n_mp, subs), out_shape=(plt...]
where the time goes in v2:
time: 46.5 us; the launch traced here: 46.1 us
  Pallas kernels  43.9 us (94%)
  local copies, waits for them, and re-layouts  1.56 us (3%)
  between operations  0.64 us (1%)
    pallas_call x1, Pallas kernels, gathered_call(): pl.pallas_call(functools.partial(gathered, n, n_mp, subs), out_shape=(plt...  43.9 us
    unnamed x2, local copies, waits for them, and re-layouts  1.56 us

profile of v2, /device:TPU:0, one launch (start us, length us, event | category | flops | bytes accessed | tf_op | source)
XLA Modules:
  0.0 46.1 jit_solution(11911647818810587987)
XLA Ops:
  0.6 43.9 %shard_map.122 = (bf16[192,1280]{1,0:T(8,128)(2,1)S(1)}, bf16[192,1280]{1,0:T(8,128)(2,1)S(1)}) custom-call(bf16[192,256]{1,0:T(8,128)(2,1)} %q_hbm.1, bf16[192,256]{1,0:T(8,128)(2,1)} %dq_hbm.1, bf16[192,256]{1,0:T(8,128)(2,1)} %k_hbm.1, bf16[192,256]{1,0:T(8,128)(2,1)} %v_hbm.1, bf16[192,256]{1,0:T(8,128)(2,1)} %dk_hbm.1, bf16[192,256]{1,0:T(8,128)(2,1)} %dv_hbm.1, ...), custom_call_target="tpu_custom_call" | custom-call | tf_op jit(solution)/shard_map/pallas_call | solution.py:871
  44.6 0.8 %copy.15 = bf16[192,1280]{1,0:T(8,128)(2,1)} copy(bf16[192,1280]{1,0:T(8,128)(2,1)S(1)} %get-tuple-element.2) | data formatting | bytes 983040
  45.4 0.8 %copy.16 = bf16[192,1280]{1,0:T(8,128)(2,1)} copy(bf16[192,1280]{1,0:T(8,128)(2,1)S(1)} %get-tuple-element.3) | data formatting | bytes 983040

commit v3 on v2

--- a/solution.py
+++ b/solution.py
@@ -402,7 +402,6 @@
 def gathered(
     n,
     n_mp,
-    subs,
     q_hbm,
     dq_hbm,
     k_hbm,
@@ -438,7 +437,6 @@
     x_sem,
     small_sem,
     w_local,
-    qs_,
     qr,
     ks,
     kr,
@@ -457,25 +455,23 @@
     rows, width = q_hbm.shape
     heads = width // HD
     cols = out.shape[1]
-    part = rows // subs
     t = lax.axis_index("tm")
     m = lax.axis_index("mp")
     z, y = t // 2, t % 2
     plane, core = m // 2, m % 2
     side = z // 2
     role = jnp.where(side == 0, 1 - z % 2, z % 2)
-    far = (side + core) % 2
     home = role == 0
-    itself = jnp.logical_and(home, jnp.logical_and(side == core, y == core))
+    itself = jnp.logical_and(home, y == core)
 
     def chip(side_, role_):
         return 2 * side_ + jnp.where(side_ == 0, 1 - role_, role_)
 
-    homes = [(2 * chip(core, 0) + j, 2 * plane + y) for j in range(heads)]
-    at_home = [jnp.logical_and(itself, y == j) for j in range(heads)]
+    order = (jnp.where(home, 1 - side, side), jnp.where(home, side, 1 - side))
+    rels = (1 - role, role)
+    homes = [(2 * chip(h, 0) + core, 2 * plane + y) for h in order]
     sources = [
-        (2 * chip((side + i // 2) % 2, i % 2) + core, 2 * plane + side)
-        for i in range(4)
+        (2 * chip((side + g // 2) % 2, g % 2) + core, 2 * plane + y) for g in range(4)
     ]
     twin = (t, 2 * plane + 1 - core)
     across = (t, 2 * (1 - plane) + core)
@@ -498,8 +494,8 @@
     def greet(dev):
         pl.semaphore_signal(barrier, inc=1, device_id=dev, device_id_type=MESH)
 
-    for j in range(heads):
-        unless(at_home[j], lambda: greet(homes[j]))
+    greet(homes[0])
+    unless(itself, lambda: greet(homes[1]))
 
     @pl.when(home)
     def _():
@@ -555,15 +551,6 @@
         4 + heads + 4 * home.astype(jnp.int32) - 2 * itself.astype(jnp.int32),
     )
 
-    def q_ends(j):
-        slot = 2 * far + role
-        return qpack.at[j], qcat.at[slot], qr.at[slot]
-
-    def kv_ends(j, sub):
-        blk = 2 * y + role
-        src = pack.at[j, :, sub * part : (sub + 1) * part]
-        return src, kv.at[far, sub, :, blk], kr.at[far, sub, blk]
-
     def remote(ends, send_sem, dev):
         src, dst, sem = ends
         return pltpu.make_async_remote_copy(
@@ -575,25 +562,28 @@
             device_id_type=MESH,
         )
 
-    def q_remote(j):
-        return remote(q_ends(j), qs_.at[j], homes[j])
-
-    def kv_remote(j, sub):
-        return remote(kv_ends(j, sub), ks.at[j, sub], homes[j])
-
-    for j in range(heads):
-        both(
-            at_home[j],
-            lambda: pltpu.make_async_copy(*q_ends(j)).start(),
-            lambda: q_remote(j).start(),
-        )
-    for sub in range(subs):
-        for j in range(heads):
-            both(
-                at_home[j],
-                lambda: pltpu.make_async_copy(*kv_ends(j, sub)).start(),
-                lambda: kv_remote(j, sub).start(),
-            )
+    def home_ends(o, piece):
+        h = order[o]
+        g = 2 * rels[o] + role
+        if piece == 0:
+            return qpack.at[h], qcat.at[g], qr.at[g]
+        pair = slice(2 * piece - 2, 2 * piece)
+        blk = 2 * g + y
+        return pack.at[h, pair], kv.at[pair, blk], kr.at[piece - 1, blk]
+
+    def home_copy(o, piece):
+        return remote(home_ends(o, piece), ks.at[o, piece], homes[o])
+
+    def home_all(o):
+        for piece in range(3):
+            home_copy(o, piece).start()
+
+    def home_local():
+        for piece in range(3):
+            pltpu.make_async_copy(*home_ends(1, piece)).start()
+
+    home_all(0)
+    both(itself, home_local, lambda: home_all(1))
 
     tile = 16
     y_rows = (width // tile * 5 // 16) * tile
@@ -652,29 +642,33 @@
     for load in x_loads:
         load.start()
 
-    def to_twin(rel, sub, i):
-        blk = 2 * core + i
-        ref = kv.at[rel, sub, :, blk]
-        return remote((ref, ref, kr.at[rel, sub, blk]), fs.at[rel, sub, i], twin)
-
-    def kv_wait(rel, sub, blk):
-        ref = kv.at[rel, sub, :, blk]
-        pltpu.make_async_copy(ref, ref, kr.at[rel, sub, blk]).wait()
-
-    def arrivals(rel, sub):
-        for i in range(2):
-            kv_wait(rel, sub, 2 * core + i)
-            to_twin(rel, sub, i).start()
-        for i in range(2):
-            kv_wait(rel, sub, 2 * (1 - core) + i)
+    def to_twin(pair, g):
+        ref = kv.at[2 * pair : 2 * pair + 2, 2 * g + core]
+        return remote((ref, ref, kr.at[pair, 2 * g + core]), fs.at[pair, g], twin)
+
+    def kv_wait(pair, blk):
+        ref = kv.at[2 * pair : 2 * pair + 2, blk]
+        pltpu.make_async_copy(ref, ref, kr.at[pair, blk]).wait()
+
+    def arrive(g):
+        for pair in range(2):
+            kv_wait(pair, 2 * g + core)
+            to_twin(pair, g).start()
+
+    def from_twin(g):
+        for pair in range(2):
+            kv_wait(pair, 2 * g + 1 - core)
 
     def q_wait(i):
         pltpu.make_async_copy(qcat.at[i], qcat.at[i], qr.at[i]).wait()
 
-    def attend(rel, sub, i):
-        first = rel == 0 and sub == 0
-        keys = 4 * part
-        k, tk, v, tv = (kv[rel, sub, p].reshape(keys, HD) for p in range(4))
+    def attend(blocks, i):
+        first = blocks[0] == 0
+        last = blocks[1] == 8
+        keys = (blocks[1] - blocks[0]) * rows
+        k, tk, v, tv = (
+            kv[p, blocks[0] : blocks[1]].reshape(keys, HD) for p in range(4)
+        )
         scores = dot_nt(qcat[i, :, HD : 2 * HD], k)
         d_scores = dot_nt(qcat[i], jnp.concatenate([k, tk], axis=1)) * factor
         peak = jnp.max(scores, axis=1, keepdims=True)
@@ -696,7 +690,7 @@
             slope = c_s[i] * rescale + slope
             primal = a_s[i] * rescale + primal
             tangent = g_s[i] * rescale + tangent
-        if rel == 1 and sub == subs - 1:
+        if last:
             inverse = 1.0 / total
             outputs = primal * inverse
             d_outputs = tangent * inverse - (slope * inverse) * outputs
@@ -710,7 +704,7 @@
             g_s[i] = tangent
 
     def res_ends(i, a):
-        return res.at[i, a], ao.at[y, 0, a], rr.at[y, a]
+        return res.at[i, a], ao.at[side, 0, a], rr.at[side, a]
 
     def res_remote(i, a):
         return remote(res_ends(i, a), rs.at[i, a], sources[i])
@@ -731,26 +725,24 @@
 
     @pl.when(home)
     def _():
-        q_wait(0)
-        q_wait(1)
-        for sub in range(subs):
-            arrivals(0, sub)
-            for i in (0, 1):
-                attend(0, sub, i)
+        arrive(0)
         w_row_relay(0)
-        q_wait(2)
-        q_wait(3)
-        for sub in range(subs):
-            for i in (2, 3):
-                attend(0, sub, i)
+        arrive(2)
+        arrive(1)
+        for g in range(3):
+            q_wait(g)
+            from_twin(g)
+        for i in range(3):
+            attend((0, 6), i)
         for piece in range(1, halves):
             w_row_relay(piece)
-        for sub in range(subs):
-            arrivals(1, sub)
-            for i in (2, 3, 0, 1):
-                attend(1, sub, i)
-                if sub == subs - 1:
-                    res_start(i)
+        q_wait(3)
+        attend((0, 6), 3)
+        arrive(3)
+        from_twin(3)
+        for i in (3, 2, 1, 0):
+            attend((6, 8), i)
+            res_start(i)
 
     @pl.when(jnp.logical_not(home))
     def _():
@@ -777,42 +769,46 @@
     chunks = [slice(c, c + step) for c in range(0, cols, step)]
 
     def project(slots, a, chunk):
-        attn = jnp.concatenate([ao[h, j, a] for h, j in slots], axis=1)
-        weight = jnp.concatenate(
-            [wbuf[j, h * HD : (h + 1) * HD, chunk] for h, j in slots], axis=0
-        )
+        attn = jnp.concatenate([ao[heads_[h], j, a] for h, j in slots], axis=1)
+        weight = jnp.concatenate([wbuf[j, w_rows[h], chunk] for h, j in slots], axis=0)
         return dot_nn(attn, weight)
 
-    own_plane = [(h, j) for j in (0, 1) for h in range(heads)]
-    other_plane = [(h, j) for j in (2, 3) for h in range(heads)]
+    heads_ = (side, 1 - side)
+    w_rows = [pl.ds(pl.multiple_of(h * HD, HD), HD) for h in heads_]
+    near, far = heads_
     for a in range(2):
-        for h in range(heads):
-            own_heads(h, a)
+        own_heads(near, a)
     w_own.wait()
     w_twin.wait_recv()
     for load in x_loads:
         load.wait()
     for a in range(2):
-        for h in range(heads):
-            ao_copy(h, 1, a).wait_recv()
-        for chunk in chunks:
-            acc[a, :, chunk] = project(own_plane, a, chunk)
+        ao_copy(near, 1, a).wait_recv()
+    for a in range(2):
+        own_heads(far, a)
     for slot in range(2):
         for piece in range(halves, 2 * halves):
             w_cross(slot, piece).wait_recv()
         for piece in range(halves):
             w_row(slot, piece).wait_recv()
     for a in range(2):
-        for h in range(heads):
-            cross_heads(h, a)
-    for h in range(heads):
-        ao_copy(h, 3, 0).wait_recv()
+        cross_heads(near, a)
+    for a in range(2):
+        ao_copy(far, 1, a).wait_recv()
+    for a in range(2):
+        for chunk in chunks:
+            acc[a, :, chunk] = project([(0, 0), (0, 1), (1, 0), (1, 1)], a, chunk)
+    for a in range(2):
+        cross_heads(far, a)
+    for a in range(2):
+        ao_copy(near, 3, a).wait_recv()
+    ao_copy(far, 3, 0).wait_recv()
+    other_plane = [(0, 2), (0, 3), (1, 2), (1, 3)]
     for chunk in chunks:
         total = acc[0, :, chunk] + project(other_plane, 0, chunk)
         scale = gate[chunk].reshape(1, step)
         out[:, chunk] = (xbuf[0, :, chunk].astype(F32) + scale * total).astype(BF16)
-    for h in range(heads):
-        ao_copy(h, 3, 1).wait_recv()
+    ao_copy(far, 3, 1).wait_recv()
     for chunk in chunks:
         total = acc[1, :, chunk] + project(other_plane, 1, chunk)
         scale = gate[chunk].reshape(1, step)
@@ -822,14 +818,12 @@
             base = base * jnp.full(base.shape, live[i], F32)
             d_out[piece, chunk] = (base + scale * total[piece]).astype(BF16)
 
-    for j in range(heads):
-
-        def sent():
-            q_remote(j).wait_send()
-            for sub in range(subs):
-                kv_remote(j, sub).wait_send()
-
-        unless(at_home[j], sent)
+    def sent(o):
+        for piece in range(3):
+            home_copy(o, piece).wait_send()
+
+    sent(0)
+    unless(itself, lambda: sent(1))
     for slot in range(2):
         for piece in range(2 * halves):
             w_cross(slot, piece).wait_send()
@@ -839,10 +833,9 @@
 
     @pl.when(home)
     def _():
-        for rel in range(2):
-            for sub in range(subs):
-                for i in range(2):
-                    to_twin(rel, sub, i).wait_send()
+        for g in range(4):
+            for pair in range(2):
+                to_twin(pair, g).wait_send()
         for i in range(1, 4):
             for a in range(2):
                 res_remote(i, a).wait_send()
@@ -863,13 +856,11 @@
     cols = x.shape[1]
     heads = width // HD
     halves = 2 if cols % (2 * HD) == 0 else 1
-    subs = 3 if rows % (3 * FRAME) == 0 else 1
-    part = rows // subs
     anywhere = pl.BlockSpec(memory_space=pl.ANY)
     vmem = pl.BlockSpec(memory_space=pltpu.VMEM)
     dma = pltpu.SemaphoreType.DMA
     return pl.pallas_call(
-        functools.partial(gathered, n, n_mp, subs),
+        functools.partial(gathered, n, n_mp),
         out_shape=(pltpu.VMEM(x.shape, BF16), pltpu.VMEM(x.shape, BF16)),
         in_specs=[anywhere] * 11,
         out_specs=(vmem, vmem),
@@ -878,7 +869,7 @@
             pltpu.VMEM((heads, rows, 2 * HD), BF16),
             pltpu.VMEM((heads, 4, rows, HD), BF16),
             pltpu.VMEM((4, rows, 2 * HD), BF16),
-            pltpu.VMEM((2, subs, 4, 4, part, HD), BF16),
+            pltpu.VMEM((4, 8, rows, HD), BF16),
             pltpu.VMEM((4, rows, 1), F32),
             pltpu.VMEM((4, rows, 1), F32),
             pltpu.VMEM((4, rows, 1), F32),
@@ -896,11 +887,10 @@
             dma((2,)),
             dma((2,)),
             dma,
-            dma((heads,)),
             dma((4,)),
-            dma((heads, subs)),
-            dma((2, subs, 4)),
-            dma((2, subs, 2)),
+            dma((heads, 3)),
+            dma((2, 8)),
+            dma((2, 4)),
             dma,
             dma,
             dma((2, 2 * halves)),

time: 46.5 us -> 45.2 us (0.972)
  Pallas kernels: 43.9 us -> 42.9 us
    pallas_call x1, Pallas kernels: 43.9 us -> 42.9 us  [gathered_call(): pl.pallas_call(functools.partial(gathered, n, n_mp), out_shape=(pltpu.VME...]
where the time goes in v3:
time: 45.2 us; the launch traced here: 45.1 us
  Pallas kernels  42.9 us (95%)
  local copies, waits for them, and re-layouts  1.56 us (3%)
  between operations  0.64 us (1%)
    pallas_call x1, Pallas kernels, gathered_call(): pl.pallas_call(functools.partial(gathered, n, n_mp), out_shape=(pltpu.VME...  42.9 us
    unnamed x2, local copies, waits for them, and re-layouts  1.56 us

profile of v3, /device:TPU:0, one launch (start us, length us, event | category | flops | bytes accessed | tf_op | source)
XLA Modules:
  0.0 45.1 jit_solution(9887004422229109167)
XLA Ops:
  0.6 42.9 %shard_map.122 = (bf16[192,1280]{1,0:T(8,128)(2,1)S(1)}, bf16[192,1280]{1,0:T(8,128)(2,1)S(1)}) custom-call(bf16[192,256]{1,0:T(8,128)(2,1)} %q_hbm.1, bf16[192,256]{1,0:T(8,128)(2,1)} %dq_hbm.1, bf16[192,256]{1,0:T(8,128)(2,1)} %k_hbm.1, bf16[192,256]{1,0:T(8,128)(2,1)} %v_hbm.1, bf16[192,256]{1,0:T(8,128)(2,1)} %dk_hbm.1, bf16[192,256]{1,0:T(8,128)(2,1)} %dv_hbm.1, ...), custom_call_target="tpu_custom_call" | custom-call | tf_op jit(solution)/shard_map/pallas_call | solution.py:862
  43.5 0.8 %copy.15 = bf16[192,1280]{1,0:T(8,128)(2,1)} copy(bf16[192,1280]{1,0:T(8,128)(2,1)S(1)} %get-tuple-element.2) | data formatting | bytes 983040
  44.3 0.8 %copy.16 = bf16[192,1280]{1,0:T(8,128)(2,1)} copy(bf16[192,1280]{1,0:T(8,128)(2,1)S(1)} %get-tuple-element.3) | data formatting | bytes 983040

commit v4 on v3

--- a/solution.py
+++ b/solution.py
@@ -418,6 +418,8 @@
     own,
     qpack,
     pack,
+    qpeer,
+    peer,
     qcat,
     kv,
     m_s,
@@ -440,6 +442,9 @@
     qr,
     ks,
     kr,
+    ps,
+    pr,
+    ts,
     fs,
     wts,
     wtr,
@@ -462,13 +467,13 @@
     side = z // 2
     role = jnp.where(side == 0, 1 - z % 2, z % 2)
     home = role == 0
-    itself = jnp.logical_and(home, y == core)
+    straight = y == core
+    itself = jnp.logical_and(home, straight)
 
     def chip(side_, role_):
         return 2 * side_ + jnp.where(side_ == 0, 1 - role_, role_)
 
-    order = (jnp.where(home, 1 - side, side), jnp.where(home, side, 1 - side))
-    rels = (1 - role, role)
+    order = (side, 1 - side)
     homes = [(2 * chip(h, 0) + core, 2 * plane + y) for h in order]
     sources = [
         (2 * chip((side + g // 2) % 2, g % 2) + core, 2 * plane + y) for g in range(4)
@@ -494,14 +499,24 @@
     def greet(dev):
         pl.semaphore_signal(barrier, inc=1, device_id=dev, device_id_type=MESH)
 
-    greet(homes[0])
-    unless(itself, lambda: greet(homes[1]))
+    greet(homes[1])
+    unless(itself, lambda: greet(homes[0]))
 
     @pl.when(home)
     def _():
         for i in (3, 2, 1):
             greet(sources[i])
         unless(itself, lambda: greet(sources[0]))
+
+    @pl.when(straight)
+    def _():
+        for h in order:
+            greet((2 * chip(h, 0) + y, 2 * plane + 1 - y))
+
+    @pl.when(jnp.logical_and(home, jnp.logical_not(straight)))
+    def _():
+        for g in range(4):
+            greet((2 * chip((side + g // 2) % 2, g % 2) + y, 2 * plane + y))
 
     for dev in (across, diagonal, row_peer, twin):
         greet(dev)
@@ -548,7 +563,9 @@
 
     pl.semaphore_wait(
         barrier,
-        4 + heads + 4 * home.astype(jnp.int32) - 2 * itself.astype(jnp.int32),
+        4 + heads + 4 * home.astype(jnp.int32) - 2 * itself.astype(jnp.int32)
+        + 2 * straight.astype(jnp.int32)
+        + 4 * (home.astype(jnp.int32) - itself.astype(jnp.int32)),
     )
 
     def remote(ends, send_sem, dev):
@@ -562,14 +579,16 @@
             device_id_type=MESH,
         )
 
-    def home_ends(o, piece):
+    def home_ends(o, piece, relayed=False):
         h = order[o]
-        g = 2 * rels[o] + role
+        g = 2 * o + role
         if piece == 0:
-            return qpack.at[h], qcat.at[g], qr.at[g]
+            return (qpeer.at[o] if relayed else qpack.at[h]), qcat.at[g], qr.at[g]
         pair = slice(2 * piece - 2, 2 * piece)
-        blk = 2 * g + y
-        return pack.at[h, pair], kv.at[pair, blk], kr.at[piece - 1, blk]
+        crossing = 1 if relayed else (y + core) % 2
+        slot = g + 4 * crossing
+        src = peer.at[o, pair] if relayed else pack.at[h, pair]
+        return src, kv.at[pair, slot], kr.at[piece - 1, slot]
 
     def home_copy(o, piece):
         return remote(home_ends(o, piece), ks.at[o, piece], homes[o])
@@ -580,10 +599,46 @@
 
     def home_local():
         for piece in range(3):
-            pltpu.make_async_copy(*home_ends(1, piece)).start()
-
-    home_all(0)
-    both(itself, home_local, lambda: home_all(1))
+            pltpu.make_async_copy(*home_ends(0, piece)).start()
+
+    def peer_copy(o, piece):
+        h = order[o]
+        if piece == 0:
+            ends = (qpack.at[h], qpeer.at[o], pr.at[o, piece])
+        else:
+            pair = slice(2 * piece - 2, 2 * piece)
+            ends = (pack.at[h, pair], peer.at[o, pair], pr.at[o, piece])
+        return remote(ends, ps.at[o, piece], row_peer)
+
+    def peer_all(o):
+        for piece in range(3):
+            peer_copy(o, piece).start()
+
+    def onward(o, piece):
+        dev = (2 * chip(order[o], 0) + y, 2 * plane + 1 - y)
+        return remote(home_ends(o, piece, True), ts.at[o, piece], dev)
+
+    def relay(o):
+        for piece in range(3):
+            peer_copy(o, piece).wait_recv()
+            onward(o, piece).start()
+
+    def straight_sends():
+        both(itself, home_local, lambda: home_all(0))
+        home_all(1)
+
+    def crossing_sends():
+        def middle():
+            peer_all(1)
+            home_all(0)
+
+        def end():
+            peer_all(0)
+            peer_all(1)
+
+        both(home, middle, end)
+
+    both(straight, straight_sends, crossing_sends)
 
     tile = 16
     y_rows = (width // tile * 5 // 16) * tile
@@ -642,22 +697,25 @@
     for load in x_loads:
         load.start()
 
+    mine_at = 4 * ((y + core) % 2)
+    twins_at = 4 - mine_at
+
     def to_twin(pair, g):
-        ref = kv.at[2 * pair : 2 * pair + 2, 2 * g + core]
-        return remote((ref, ref, kr.at[pair, 2 * g + core]), fs.at[pair, g], twin)
-
-    def kv_wait(pair, blk):
-        ref = kv.at[2 * pair : 2 * pair + 2, blk]
-        pltpu.make_async_copy(ref, ref, kr.at[pair, blk]).wait()
+        ref = kv.at[2 * pair : 2 * pair + 2, g + mine_at]
+        return remote((ref, ref, kr.at[pair, g + mine_at]), fs.at[pair, g], twin)
+
+    def kv_wait(pair, slot):
+        ref = kv.at[2 * pair : 2 * pair + 2, slot]
+        pltpu.make_async_copy(ref, ref, kr.at[pair, slot]).wait()
 
     def arrive(g):
         for pair in range(2):
-            kv_wait(pair, 2 * g + core)
+            kv_wait(pair, g + mine_at)
             to_twin(pair, g).start()
 
     def from_twin(g):
         for pair in range(2):
-            kv_wait(pair, 2 * g + 1 - core)
+            kv_wait(pair, g + twins_at)
 
     def q_wait(i):
         pltpu.make_async_copy(qcat.at[i], qcat.at[i], qr.at[i]).wait()
@@ -725,27 +783,46 @@
 
     @pl.when(home)
     def _():
-        arrive(0)
+        def early_straight():
+            relay(1)
+            for g in range(4):
+                arrive(g)
+            from_twin(0)
+
+        def early_crossing():
+            arrive(0)
+            for g in range(4):
+                from_twin(g)
+
+        def late_straight():
+            for g in range(1, 4):
+                from_twin(g)
+
+        def late_crossing():
+            for g in range(1, 4):
+                arrive(g)
+
+        both(straight, early_straight, early_crossing)
+        q_wait(0)
+        attend((0, 5), 0)
         w_row_relay(0)
-        arrive(2)
-        arrive(1)
-        for g in range(3):
+        for g in range(1, 4):
             q_wait(g)
-            from_twin(g)
-        for i in range(3):
-            attend((0, 6), i)
+            attend((0, 5), g)
         for piece in range(1, halves):
             w_row_relay(piece)
-        q_wait(3)
-        attend((0, 6), 3)
-        arrive(3)
-        from_twin(3)
+        both(straight, late_straight, late_crossing)
         for i in (3, 2, 1, 0):
-            attend((6, 8), i)
+            attend((5, 8), i)
             res_start(i)
 
     @pl.when(jnp.logical_not(home))
     def _():
+        @pl.when(straight)
+        def _():
+            relay(0)
+            relay(1)
+
         for piece in range(halves):
             w_row_relay(piece)
 
@@ -776,54 +853,71 @@
     heads_ = (side, 1 - side)
     w_rows = [pl.ds(pl.multiple_of(h * HD, HD), HD) for h in heads_]
     near, far = heads_
-    for a in range(2):
-        own_heads(near, a)
+
+    def own_plane(a):
+        for h in heads_:
+            ao_copy(h, 1, a).wait_recv()
+        for chunk in chunks:
+            acc[a, :, chunk] = project([(0, 0), (0, 1), (1, 0), (1, 1)], a, chunk)
+
+    def other_plane(a, result):
+        for h in heads_:
+            ao_copy(h, 3, a).wait_recv()
+        slots = [(0, 2), (0, 3), (1, 2), (1, 3)]
+        for chunk in chunks:
+            total = acc[a, :, chunk] + project(slots, a, chunk)
+            scale = gate[chunk].reshape(1, step)
+            base = xbuf[a, :, chunk].astype(F32)
+            result[:, chunk] = (base + scale * total).astype(BF16)
+
     w_own.wait()
     w_twin.wait_recv()
     for load in x_loads:
         load.wait()
-    for a in range(2):
-        ao_copy(near, 1, a).wait_recv()
-    for a in range(2):
-        own_heads(far, a)
+    for i in range(rows // FRAME):
+        piece = slice(i * FRAME, (i + 1) * FRAME)
+        xbuf[1, piece] = masked(xbuf[1, piece], i)
+    for h in heads_:
+        own_heads(h, 0)
+    own_plane(0)
+    for h in heads_:
+        own_heads(h, 1)
     for slot in range(2):
         for piece in range(halves, 2 * halves):
             w_cross(slot, piece).wait_recv()
         for piece in range(halves):
             w_row(slot, piece).wait_recv()
-    for a in range(2):
-        cross_heads(near, a)
-    for a in range(2):
-        ao_copy(far, 1, a).wait_recv()
-    for a in range(2):
-        for chunk in chunks:
-            acc[a, :, chunk] = project([(0, 0), (0, 1), (1, 0), (1, 1)], a, chunk)
-    for a in range(2):
-        cross_heads(far, a)
-    for a in range(2):
-        ao_copy(near, 3, a).wait_recv()
-    ao_copy(far, 3, 0).wait_recv()
-    other_plane = [(0, 2), (0, 3), (1, 2), (1, 3)]
-    for chunk in chunks:
-        total = acc[0, :, chunk] + project(other_plane, 0, chunk)
-        scale = gate[chunk].reshape(1, step)
-        out[:, chunk] = (xbuf[0, :, chunk].astype(F32) + scale * total).astype(BF16)
-    ao_copy(far, 3, 1).wait_recv()
-    for chunk in chunks:
-        total = acc[1, :, chunk] + project(other_plane, 1, chunk)
-        scale = gate[chunk].reshape(1, step)
-        for i in range(rows // FRAME):
-            piece = slice(i * FRAME, (i + 1) * FRAME)
-            base = xbuf[1, piece, chunk].astype(F32)
-            base = base * jnp.full(base.shape, live[i], F32)
-            d_out[piece, chunk] = (base + scale * total[piece]).astype(BF16)
+    for h in heads_:
+        cross_heads(h, 0)
+    own_plane(1)
+    for h in heads_:
+        cross_heads(h, 1)
+    other_plane(0, out)
+    other_plane(1, d_out)
 
     def sent(o):
         for piece in range(3):
             home_copy(o, piece).wait_send()
 
-    sent(0)
-    unless(itself, lambda: sent(1))
+    def peers_sent(o):
+        for piece in range(3):
+            peer_copy(o, piece).wait_send()
+
+    def relays_sent(o):
+        for piece in range(3):
+            onward(o, piece).wait_send()
+
+    def straight_sent():
+        sent(1)
+        unless(itself, lambda: sent(0))
+        relays_sent(1)
+        unless(home, lambda: relays_sent(0))
+
+    def crossing_sent():
+        peers_sent(1)
+        both(home, lambda: sent(0), lambda: peers_sent(0))
+
+    both(straight, straight_sent, crossing_sent)
     for slot in range(2):
         for piece in range(2 * halves):
             w_cross(slot, piece).wait_send()
@@ -866,6 +960,8 @@
         out_specs=(vmem, vmem),
         scratch_shapes=[
             pltpu.VMEM((3, rows, width), BF16),
+            pltpu.VMEM((heads, rows, 2 * HD), BF16),
+            pltpu.VMEM((heads, 4, rows, HD), BF16),
             pltpu.VMEM((heads, rows, 2 * HD), BF16),
             pltpu.VMEM((heads, 4, rows, HD), BF16),
             pltpu.VMEM((4, rows, 2 * HD), BF16),
@@ -890,6 +986,9 @@
             dma((4,)),
             dma((heads, 3)),
             dma((2, 8)),
+            dma((heads, 3)),
+            dma((heads, 3)),
+            dma((heads, 3)),
             dma((2, 4)),
             dma,
             dma,

time: 45.2 us -> 38.3 us (0.85)
  Pallas kernels: 42.9 us -> 35.8 us
    pallas_call x1, Pallas kernels: 42.9 us -> 35.8 us  [gathered_call(): pl.pallas_call(functools.partial(gathered, n, n_mp), out_shape=(pltpu.VME...]
where the time goes in v4:
time: 38.3 us; the launch traced here: 38 us
  Pallas kernels  35.8 us (93%)
  local copies, waits for them, and re-layouts  1.56 us (4%)
  between operations  0.64 us (2%)
    pallas_call x1, Pallas kernels, gathered_call(): pl.pallas_call(functools.partial(gathered, n, n_mp), out_shape=(pltpu.VME...  35.8 us
    unnamed x2, local copies, waits for them, and re-layouts  1.56 us

profile of v4, /device:TPU:0, one launch (start us, length us, event | category | flops | bytes accessed | tf_op | source)
XLA Modules:
  0.0 38.0 jit_solution(4359681838610836273)
XLA Ops:
  0.6 35.8 %shard_map.122 = (bf16[192,1280]{1,0:T(8,128)(2,1)S(1)}, bf16[192,1280]{1,0:T(8,128)(2,1)S(1)}) custom-call(bf16[192,256]{1,0:T(8,128)(2,1)} %q_hbm.1, bf16[192,256]{1,0:T(8,128)(2,1)} %dq_hbm.1, bf16[192,256]{1,0:T(8,128)(2,1)} %k_hbm.1, bf16[192,256]{1,0:T(8,128)(2,1)} %v_hbm.1, bf16[192,256]{1,0:T(8,128)(2,1)} %dk_hbm.1, bf16[192,256]{1,0:T(8,128)(2,1)} %dv_hbm.1, ...), custom_call_target="tpu_custom_call" | custom-call | tf_op jit(solution)/shard_map/pallas_call | solution.py:956
  36.4 0.8 %copy.15 = bf16[192,1280]{1,0:T(8,128)(2,1)} copy(bf16[192,1280]{1,0:T(8,128)(2,1)S(1)} %get-tuple-element.2) | data formatting | bytes 983040
  37.2 0.8 %copy.16 = bf16[192,1280]{1,0:T(8,128)(2,1)} copy(bf16[192,1280]{1,0:T(8,128)(2,1)S(1)} %get-tuple-element.3) | data formatting | bytes 983040

commit v5 on v4

--- a/solution.py
+++ b/solution.py
@@ -434,17 +434,14 @@
     xbuf,
     flags,
     gate,
-    own_sem,
     raw_sem,
     x_sem,
     small_sem,
     w_local,
     qr,
-    ks,
+    zs,
     kr,
-    ps,
     pr,
-    ts,
     fs,
     wts,
     wtr,
@@ -483,6 +480,7 @@
     diagonal = (t, 2 * (1 - plane) + 1 - core)
     row_peer = (2 * z + 1 - y, m)
     factor = 1.0 / math.sqrt(HD)
+    power = factor * math.log2(math.e)
 
     def lanes(h):
         return slice(h * HD, (h + 1) * HD)
@@ -522,11 +520,15 @@
         greet(dev)
 
     loads = [
-        pltpu.make_async_copy(src, own.at[i], own_sem.at[i])
+        pltpu.make_async_copy(src, own.at[i], raw_sem)
         for i, src in enumerate((dq_hbm, dk_hbm, dv_hbm))
     ]
-    loads.append(pltpu.make_async_copy(flags_hbm, flags, small_sem.at[0]))
+    flags_load = pltpu.make_async_copy(flags_hbm, flags, small_sem.at[0])
     raw = []
+
+    def done(ref, sem):
+        pltpu.make_async_copy(ref, ref, sem).wait()
+
     for j in range(heads):
         for i, (src, dst) in enumerate(
             (
@@ -536,12 +538,13 @@
             )
         ):
             raw.append(
-                pltpu.make_async_copy(src.at[:, lanes(j)], dst, raw_sem.at[j, i])
+                pltpu.make_async_copy(src.at[:, lanes(j)], dst, raw_sem)
             )
+    flags_load.start()
     for load in loads + raw:
         load.start()
-    for load in loads:
-        load.wait()
+    flags_load.wait()
+    done(kv.at[0:4, 0:3], raw_sem)
 
     live = [
         jnp.where(flags[i * FRAME] > 0, 1.0, 0.0).astype(F32)
@@ -558,9 +561,6 @@
             qpack[h, piece, 0:HD] = masked(own[0, piece, lanes(h)], i)
             pack[h, 1, piece] = masked(own[1, piece, lanes(h)], i)
             pack[h, 3, piece] = masked(own[2, piece, lanes(h)], i)
-    for load in raw:
-        load.wait()
-
     pl.semaphore_wait(
         barrier,
         4 + heads + 4 * home.astype(jnp.int32) - 2 * itself.astype(jnp.int32)
@@ -591,7 +591,7 @@
         return src, kv.at[pair, slot], kr.at[piece - 1, slot]
 
     def home_copy(o, piece):
-        return remote(home_ends(o, piece), ks.at[o, piece], homes[o])
+        return remote(home_ends(o, piece), zs, homes[o])
 
     def home_all(o):
         for piece in range(3):
@@ -608,7 +608,7 @@
         else:
             pair = slice(2 * piece - 2, 2 * piece)
             ends = (pack.at[h, pair], peer.at[o, pair], pr.at[o, piece])
-        return remote(ends, ps.at[o, piece], row_peer)
+        return remote(ends, zs, row_peer)
 
     def peer_all(o):
         for piece in range(3):
@@ -616,7 +616,7 @@
 
     def onward(o, piece):
         dev = (2 * chip(order[o], 0) + y, 2 * plane + 1 - y)
-        return remote(home_ends(o, piece, True), ts.at[o, piece], dev)
+        return remote(home_ends(o, piece, True), zs, dev)
 
     def relay(o):
         for piece in range(3):
@@ -641,7 +641,7 @@
     both(straight, straight_sends, crossing_sends)
 
     tile = 16
-    y_rows = (width // tile * 5 // 16) * tile
+    y_rows = (width // tile // 4) * tile
     rest = slice(2 * y_rows, width)
     halves = 2 if cols % (2 * HD) == 0 else 1
     span = cols // halves
@@ -664,15 +664,15 @@
             (
                 w_hbm.at[rows_, w_cols(dev[1], first, size)],
                 wbuf.at[2 + slot, rows_, pl.ds(first, size)],
-                wxr.at[slot, piece],
+                wxr.at[2 * piece + slot if piece < halves else 2 * halves],
             ),
-            wxs.at[slot, piece],
+            wxs,
             dev,
         )
 
     def w_row(slot, piece):
         ref = wbuf.at[2 + slot, y_part(y), pl.ds(piece * span, span)]
-        return remote((ref, ref, wyr.at[slot, piece]), wys.at[slot, piece], row_peer)
+        return remote((ref, ref, wyr), wys, row_peer)
 
     def w_row_relay(piece):
         for slot in range(2):
@@ -690,19 +690,20 @@
     w_twin.start()
     w_own.start()
     x_loads = [
-        pltpu.make_async_copy(src, xbuf.at[i], x_sem.at[i])
+        pltpu.make_async_copy(src, xbuf.at[i], x_sem)
         for i, src in enumerate((x_hbm, dx_hbm))
     ]
-    x_loads.append(pltpu.make_async_copy(gate_hbm, gate, small_sem.at[1]))
+    gate_load = pltpu.make_async_copy(gate_hbm, gate, small_sem.at[1])
     for load in x_loads:
         load.start()
+    gate_load.start()
 
     mine_at = 4 * ((y + core) % 2)
     twins_at = 4 - mine_at
 
     def to_twin(pair, g):
         ref = kv.at[2 * pair : 2 * pair + 2, g + mine_at]
-        return remote((ref, ref, kr.at[pair, g + mine_at]), fs.at[pair, g], twin)
+        return remote((ref, ref, kr.at[pair, g + mine_at]), fs, twin)
 
     def kv_wait(pair, slot):
         ref = kv.at[2 * pair : 2 * pair + 2, slot]
@@ -720,61 +721,68 @@
     def q_wait(i):
         pltpu.make_async_copy(qcat.at[i], qcat.at[i], qr.at[i]).wait()
 
-    def attend(blocks, i):
+    def attend(blocks, queries):
         first = blocks[0] == 0
         last = blocks[1] == 8
         keys = (blocks[1] - blocks[0]) * rows
+        count = (queries[1] - queries[0]) * rows
+        at = slice(queries[0] * rows, queries[1] * rows)
+
+        def spread(column):
+            return jnp.broadcast_to(column, (count, HD))
+
         k, tk, v, tv = (
             kv[p, blocks[0] : blocks[1]].reshape(keys, HD) for p in range(4)
         )
-        scores = dot_nt(qcat[i, :, HD : 2 * HD], k)
-        d_scores = dot_nt(qcat[i], jnp.concatenate([k, tk], axis=1)) * factor
-        peak = jnp.max(scores, axis=1, keepdims=True)
+        q = qcat[queries[0] : queries[1]].reshape(count, 2 * HD)
+        scores = dot_nt(q[:, HD : 2 * HD], k)
+        d_scores = dot_nt(q, jnp.concatenate([k, tk], axis=1))
+        peak = spread(jnp.max(scores, axis=1, keepdims=True))
         if not first:
-            peak_old = m_s[i]
+            peak_old = m_s[at]
             peak = jnp.maximum(peak_old, peak)
-            rescale = jnp.exp((peak_old - peak) * factor)
-        weights = jnp.exp((scores - peak) * factor)
+            rescale = jnp.exp2((peak_old - peak) * power)
+        weights = jnp.exp2((scores - jnp.tile(peak, (1, keys // HD))) * power)
         product = weights * d_scores
-        total = jnp.sum(weights, axis=1, keepdims=True)
-        slope = jnp.sum(product, axis=1, keepdims=True)
+        total = spread(jnp.sum(weights, axis=1, keepdims=True))
+        slope = spread(jnp.sum(product, axis=1, keepdims=True))
         weights_b = weights.astype(BF16)
         product_b = product.astype(BF16)
         wide = dot_nn(weights_b, jnp.concatenate([v, tv], axis=1))
         primal = wide[:, 0:HD]
-        tangent = dot_nn(product_b, v) + wide[:, HD : 2 * HD]
+        tangent = dot_nn(product_b, v) * factor + wide[:, HD : 2 * HD]
         if not first:
-            total = l_s[i] * rescale + total
-            slope = c_s[i] * rescale + slope
-            primal = a_s[i] * rescale + primal
-            tangent = g_s[i] * rescale + tangent
+            total = l_s[at] * rescale + total
+            slope = c_s[at] * rescale + slope
+            primal = a_s[at] * rescale + primal
+            tangent = g_s[at] * rescale + tangent
         if last:
             inverse = 1.0 / total
             outputs = primal * inverse
-            d_outputs = tangent * inverse - (slope * inverse) * outputs
-            res[i, 0] = outputs.astype(BF16)
-            res[i, 1] = d_outputs.astype(BF16)
+            d_outputs = tangent * inverse - (slope * (factor * inverse)) * outputs
+            for i in range(*queries):
+                own_rows = slice((i - queries[0]) * rows, (i - queries[0] + 1) * rows)
+                res[i, 0] = outputs[own_rows].astype(BF16)
+                res[i, 1] = d_outputs[own_rows].astype(BF16)
         else:
-            m_s[i] = peak
-            l_s[i] = total
-            c_s[i] = slope
-            a_s[i] = primal
-            g_s[i] = tangent
+            m_s[at] = peak
+            l_s[at] = total
+            c_s[at] = slope
+            a_s[at] = primal
+            g_s[at] = tangent
 
     def res_ends(i, a):
         return res.at[i, a], ao.at[side, 0, a], rr.at[side, a]
 
     def res_remote(i, a):
-        return remote(res_ends(i, a), rs.at[i, a], sources[i])
-
-    def res_start(i):
+        return remote(res_ends(i, a), rs, sources[i])
+
+    def res_start(i, a):
         def local():
-            for a in range(2):
-                pltpu.make_async_copy(*res_ends(i, a)).start()
+            pltpu.make_async_copy(*res_ends(i, a)).start()
 
         def away():
-            for a in range(2):
-                res_remote(i, a).start()
+            res_remote(i, a).start()
 
         if i == 0:
             both(itself, local, away)
@@ -783,38 +791,36 @@
 
     @pl.when(home)
     def _():
-        def early_straight():
-            relay(1)
-            for g in range(4):
-                arrive(g)
-            from_twin(0)
-
-        def early_crossing():
-            arrive(0)
-            for g in range(4):
-                from_twin(g)
-
-        def late_straight():
-            for g in range(1, 4):
-                from_twin(g)
-
-        def late_crossing():
-            for g in range(1, 4):
-                arrive(g)
-
-        both(straight, early_straight, early_crossing)
+        def nothing(g):
+            pass
+
+        def each(groups, on_straight, on_crossing):
+            for g in groups:
+                both(straight, lambda: on_straight(g), lambda: on_crossing(g))
+
+        pl.when(straight)(lambda: relay(1))
+        unless(straight, lambda: arrive(0))
+        each(range(4), arrive, from_twin)
         q_wait(0)
-        attend((0, 5), 0)
+        q_wait(1)
+        attend((0, 4), (0, 2))
         w_row_relay(0)
-        for g in range(1, 4):
-            q_wait(g)
-            attend((0, 5), g)
+        each((1,), nothing, arrive)
+        q_wait(2)
+        q_wait(3)
+        attend((0, 4), (2, 4))
         for piece in range(1, halves):
             w_row_relay(piece)
-        both(straight, late_straight, late_crossing)
-        for i in (3, 2, 1, 0):
-            attend((5, 8), i)
-            res_start(i)
+        each((0, 1), from_twin, nothing)
+        each((2,), nothing, arrive)
+        attend((4, 6), (0, 4))
+        each((2,), from_twin, nothing)
+        each((3,), from_twin, arrive)
+        for queries in ((2, 4), (0, 2)):
+            attend((6, 8), queries)
+            for a in range(2):
+                for i in range(queries[1] - 1, queries[0] - 1, -1):
+                    res_start(i, a)
 
     @pl.when(jnp.logical_not(home))
     def _():
@@ -830,7 +836,8 @@
         src = ao.at[h, 2 if j == 3 else 0, a]
         dst = ao.at[h, j, a]
         dev = across if j == 2 else twin
-        return remote((src, dst, ar.at[h, j, a]), as_.at[h, j, a], dev)
+        at = 4 * a + (2 + h if j == 2 else j // 2)
+        return remote((src, dst, ar.at[at]), as_, dev)
 
     def own_heads(h, a):
         ref = ao.at[h, 0, a]
@@ -855,14 +862,12 @@
     near, far = heads_
 
     def own_plane(a):
-        for h in heads_:
-            ao_copy(h, 1, a).wait_recv()
+        done(ao.at[:, 1, a], ar.at[4 * a])
         for chunk in chunks:
             acc[a, :, chunk] = project([(0, 0), (0, 1), (1, 0), (1, 1)], a, chunk)
 
     def other_plane(a, result):
-        for h in heads_:
-            ao_copy(h, 3, a).wait_recv()
+        done(ao.at[:, 3, a], ar.at[4 * a + 1])
         slots = [(0, 2), (0, 3), (1, 2), (1, 3)]
         for chunk in chunks:
             total = acc[a, :, chunk] + project(slots, a, chunk)
@@ -872,77 +877,43 @@
 
     w_own.wait()
     w_twin.wait_recv()
-    for load in x_loads:
-        load.wait()
+    done(xbuf, x_sem)
+    gate_load.wait()
     for i in range(rows // FRAME):
         piece = slice(i * FRAME, (i + 1) * FRAME)
         xbuf[1, piece] = masked(xbuf[1, piece], i)
-    for h in heads_:
-        own_heads(h, 0)
+    for a in range(2):
+        for h in heads_:
+            own_heads(h, a)
     own_plane(0)
-    for h in heads_:
-        own_heads(h, 1)
-    for slot in range(2):
-        for piece in range(halves, 2 * halves):
-            w_cross(slot, piece).wait_recv()
-        for piece in range(halves):
-            w_row(slot, piece).wait_recv()
+    done(wbuf.at[2:4, rest], wxr.at[2 * halves])
+    done(wbuf.at[2:4, y_part(1 - y)], wyr)
+    both(
+        jnp.logical_and(straight, jnp.logical_not(home)),
+        lambda: done(kv.at[0:4, 0:6], zs),
+        lambda: done(kv.at[0:2, 0:6], zs),
+    )
+    done(wbuf.at[0:2, 0 : width - y_rows], wxs)
+    done(wbuf.at[2:4, y_part(y)], wys)
+    w_twin.wait_send()
+
+    @pl.when(home)
+    def _():
+        done(kv.at[0:2, 0:8], fs)
+
     for h in heads_:
         cross_heads(h, 0)
     own_plane(1)
     for h in heads_:
         cross_heads(h, 1)
+    @pl.when(home)
+    def _():
+        both(itself, lambda: done(res.at[0:3], rs), lambda: done(res, rs))
+
     other_plane(0, out)
     other_plane(1, d_out)
 
-    def sent(o):
-        for piece in range(3):
-            home_copy(o, piece).wait_send()
-
-    def peers_sent(o):
-        for piece in range(3):
-            peer_copy(o, piece).wait_send()
-
-    def relays_sent(o):
-        for piece in range(3):
-            onward(o, piece).wait_send()
-
-    def straight_sent():
-        sent(1)
-        unless(itself, lambda: sent(0))
-        relays_sent(1)
-        unless(home, lambda: relays_sent(0))
-
-    def crossing_sent():
-        peers_sent(1)
-        both(home, lambda: sent(0), lambda: peers_sent(0))
-
-    both(straight, straight_sent, crossing_sent)
-    for slot in range(2):
-        for piece in range(2 * halves):
-            w_cross(slot, piece).wait_send()
-        for piece in range(halves):
-            w_row(slot, piece).wait_send()
-    w_twin.wait_send()
-
-    @pl.when(home)
-    def _():
-        for g in range(4):
-            for pair in range(2):
-                to_twin(pair, g).wait_send()
-        for i in range(1, 4):
-            for a in range(2):
-                res_remote(i, a).wait_send()
-
-        @pl.when(jnp.logical_not(itself))
-        def _():
-            for a in range(2):
-                res_remote(0, a).wait_send()
-
-    for h in range(heads):
-        for j in range(1, n_mp):
-            for a in range(2):
-                ao_copy(h, j, a).wait_send()
+    done(ao.at[:, 1:n_mp], as_)
 
 
 def gathered_call(n, n_mp, q, dq, k, v, dk, dv, flags, w, gate, x, dx):
@@ -966,11 +937,11 @@
             pltpu.VMEM((heads, 4, rows, HD), BF16),
             pltpu.VMEM((4, rows, 2 * HD), BF16),
             pltpu.VMEM((4, 8, rows, HD), BF16),
-            pltpu.VMEM((4, rows, 1), F32),
-            pltpu.VMEM((4, rows, 1), F32),
-            pltpu.VMEM((4, rows, 1), F32),
-            pltpu.VMEM((4, rows, HD), F32),
-            pltpu.VMEM((4, rows, HD), F32),
+            pltpu.VMEM((4 * rows, HD), F32),
+            pltpu.VMEM((4 * rows, HD), F32),
+            pltpu.VMEM((4 * rows, HD), F32),
+            pltpu.VMEM((4 * rows, HD), F32),
+            pltpu.VMEM((4 * rows, HD), F32),
             pltpu.VMEM((4, 2, rows, HD), BF16),
             pltpu.VMEM((heads, n_mp, 2, rows, HD), BF16),
             pltpu.VMEM((n_mp, width, cols), BF16),
@@ -978,28 +949,25 @@
             pltpu.VMEM((2, rows, cols), BF16),
             pltpu.SMEM((rows,), jnp.int32),
             pltpu.VMEM((cols,), F32),
-            dma((3,)),
-            dma((heads, 3)),
+            dma,
+            dma,
             dma((2,)),
-            dma((2,)),
             dma,
             dma((4,)),
-            dma((heads, 3)),
+            dma,
             dma((2, 8)),
             dma((heads, 3)),
-            dma((heads, 3)),
-            dma((heads, 3)),
-            dma((2, 4)),
-            dma,
-            dma,
-            dma((2, 2 * halves)),
-            dma((2, 2 * halves)),
-            dma((2, halves)),
-            dma((2, halves)),
-            dma((4, 2)),
+            dma,
+            dma,
+            dma,
+            dma,
+            dma((2 * halves + 1,)),
+            dma,
+            dma,
+            dma,
             dma((heads, 2)),
-            dma((heads, n_mp, 2)),
-            dma((heads, n_mp, 2)),
+            dma,
+            dma((8,)),
         ],
         compiler_params=pltpu.CompilerParams(
             collective_id=0, has_side_effects=True, vmem_limit_bytes=65000000

time: 38.3 us -> 37 us (0.966)
  Pallas kernels: 35.8 us -> 34.4 us
    pallas_call x1, Pallas kernels: 35.8 us -> 34.4 us  [gathered_call(): pl.pallas_call(functools.partial(gathered, n, n_mp), out_shape=(pltpu.VME...]
where the time goes in v5:
time: 37 us; the launch traced here: 36.6 us
  Pallas kernels  34.4 us (93%)
  local copies, waits for them, and re-layouts  1.56 us (4%)
  between operations  0.64 us (2%)
    pallas_call x1, Pallas kernels, gathered_call(): pl.pallas_call(functools.partial(gathered, n, n_mp), out_shape=(pltpu.VME...  34.4 us
    unnamed x2, local copies, waits for them, and re-layouts  1.56 us

profile of v5, /device:TPU:0, one launch (start us, length us, event | category | flops | bytes accessed | tf_op | source)
XLA Modules:
  0.0 36.6 jit_solution(13786883654533261222)
XLA Ops:
  0.6 34.4 %shard_map.122 = (bf16[192,1280]{1,0:T(8,128)(2,1)S(1)}, bf16[192,1280]{1,0:T(8,128)(2,1)S(1)}) custom-call(bf16[192,256]{1,0:T(8,128)(2,1)} %q_hbm.1, bf16[192,256]{1,0:T(8,128)(2,1)} %dq_hbm.1, bf16[192,256]{1,0:T(8,128)(2,1)} %k_hbm.1, bf16[192,256]{1,0:T(8,128)(2,1)} %v_hbm.1, bf16[192,256]{1,0:T(8,128)(2,1)} %dk_hbm.1, bf16[192,256]{1,0:T(8,128)(2,1)} %dv_hbm.1, ...), custom_call_target="tpu_custom_call" | custom-call | tf_op jit(solution)/shard_map/pallas_call | solution.py:927
  35.0 0.8 %copy.15 = bf16[192,1280]{1,0:T(8,128)(2,1)} copy(bf16[192,1280]{1,0:T(8,128)(2,1)S(1)} %get-tuple-element.2) | data formatting | bytes 983040
  35.8 0.8 %copy.16 = bf16[192,1280]{1,0:T(8,128)(2,1)} copy(bf16[192,1280]{1,0:T(8,128)(2,1)S(1)} %get-tuple-element.3) | data formatting | bytes 983040

commit v6 on v5

--- a/solution.py
+++ b/solution.py
@@ -641,7 +641,7 @@
     both(straight, straight_sends, crossing_sends)
 
     tile = 16
-    y_rows = (width // tile // 4) * tile
+    y_rows = (width // tile * 3 // 8) * tile
     rest = slice(2 * y_rows, width)
     halves = 2 if cols % (2 * HD) == 0 else 1
     span = cols // halves
@@ -800,22 +800,21 @@
 
         pl.when(straight)(lambda: relay(1))
         unless(straight, lambda: arrive(0))
-        each(range(4), arrive, from_twin)
+        each((0, 1), arrive, from_twin)
+        w_row_relay(0)
+        each((2, 3), arrive, from_twin)
         q_wait(0)
         q_wait(1)
         attend((0, 4), (0, 2))
-        w_row_relay(0)
-        each((1,), nothing, arrive)
+        each((0,), from_twin, nothing)
+        each((1,), from_twin, arrive)
+        attend((4, 6), (0, 2))
+        for piece in range(1, halves):
+            w_row_relay(piece)
         q_wait(2)
         q_wait(3)
-        attend((0, 4), (2, 4))
-        for piece in range(1, halves):
-            w_row_relay(piece)
-        each((0, 1), from_twin, nothing)
-        each((2,), nothing, arrive)
-        attend((4, 6), (0, 4))
-        each((2,), from_twin, nothing)
-        each((3,), from_twin, arrive)
+        attend((0, 6), (2, 4))
+        each((2, 3), from_twin, arrive)
         for queries in ((2, 4), (0, 2)):
             attend((6, 8), queries)
             for a in range(2):
@@ -859,7 +858,8 @@
 
     heads_ = (side, 1 - side)
     w_rows = [pl.ds(pl.multiple_of(h * HD, HD), HD) for h in heads_]
-    near, far = heads_
+    first = jnp.where(home, side, 1 - side)
+    second = 1 - first
 
     def own_plane(a):
         done(ao.at[:, 1, a], ar.at[4 * a])
@@ -882,8 +882,8 @@
     for i in range(rows // FRAME):
         piece = slice(i * FRAME, (i + 1) * FRAME)
         xbuf[1, piece] = masked(xbuf[1, piece], i)
-    for a in range(2):
-        for h in heads_:
+    for h in (first, second):
+        for a in range(2):
             own_heads(h, a)
     own_plane(0)
     done(wbuf.at[2:4, rest], wxr.at[2 * halves])
@@ -901,11 +901,11 @@
     def _():
         done(kv.at[0:2, 0:8], fs)
 
-    for h in heads_:
-        cross_heads(h, 0)
+    cross_heads(first, 0)
     own_plane(1)
-    for h in heads_:
-        cross_heads(h, 1)
+    cross_heads(first, 1)
+    cross_heads(second, 0)
+    cross_heads(second, 1)
     @pl.when(home)
     def _():
         both(itself, lambda: done(res.at[0:3], rs), lambda: done(res, rs))

time: 37 us -> 36.3 us (0.981)
  Pallas kernels: 34.4 us -> 33.7 us
    pallas_call x1, Pallas kernels: 34.4 us -> 33.7 us  [gathered_call(): pl.pallas_call(functools.partial(gathered, n, n_mp), out_shape=(pltpu.VME...]
where the time goes in v6:
time: 36.3 us; the launch traced here: 35.9 us
  Pallas kernels  33.7 us (93%)
  local copies, waits for them, and re-layouts  1.56 us (4%)
  between operations  0.64 us (2%)
    pallas_call x1, Pallas kernels, gathered_call(): pl.pallas_call(functools.partial(gathered, n, n_mp), out_shape=(pltpu.VME...  33.7 us
    unnamed x2, local copies, waits for them, and re-layouts  1.56 us

profile of v6, /device:TPU:0, one launch (start us, length us, event | category | flops | bytes accessed | tf_op | source)
XLA Modules:
  0.0 35.9 jit_solution(5261491407804061227)
XLA Ops:
  0.6 33.7 %shard_map.122 = (bf16[192,1280]{1,0:T(8,128)(2,1)S(1)}, bf16[192,1280]{1,0:T(8,128)(2,1)S(1)}) custom-call(bf16[192,256]{1,0:T(8,128)(2,1)} %q_hbm.1, bf16[192,256]{1,0:T(8,128)(2,1)} %dq_hbm.1, bf16[192,256]{1,0:T(8,128)(2,1)} %k_hbm.1, bf16[192,256]{1,0:T(8,128)(2,1)} %v_hbm.1, bf16[192,256]{1,0:T(8,128)(2,1)} %dk_hbm.1, bf16[192,256]{1,0:T(8,128)(2,1)} %dv_hbm.1, ...), custom_call_target="tpu_custom_call" | custom-call | tf_op jit(solution)/shard_map/pallas_call | solution.py:927
  34.4 0.8 %copy.15 = bf16[192,1280]{1,0:T(8,128)(2,1)} copy(bf16[192,1280]{1,0:T(8,128)(2,1)S(1)} %get-tuple-element.2) | data formatting | bytes 983040
  35.2 0.8 %copy.16 = bf16[192,1280]{1,0:T(8,128)(2,1)} copy(bf16[192,1280]{1,0:T(8,128)(2,1)S(1)} %get-tuple-element.3) | data formatting | bytes 983040

commit v7 on v6

--- a/solution.py
+++ b/solution.py
@@ -641,7 +641,7 @@
     both(straight, straight_sends, crossing_sends)
 
     tile = 16
-    y_rows = (width // tile * 3 // 8) * tile
+    y_rows = (width // tile * 5 // 16) * tile
     rest = slice(2 * y_rows, width)
     halves = 2 if cols % (2 * HD) == 0 else 1
     span = cols // halves
@@ -771,18 +771,26 @@
             a_s[at] = primal
             g_s[at] = tangent
 
-    def res_ends(i, a):
-        return res.at[i, a], ao.at[side, 0, a], rr.at[side, a]
-
-    def res_remote(i, a):
-        return remote(res_ends(i, a), rs, sources[i])
-
-    def res_start(i, a):
+    def part_of(p):
+        half = rows // 2
+        return p // 2, slice(p % 2 * half, (p % 2 + 1) * half)
+
+    def res_ends(i, p):
+        return (
+            res.at[i, *part_of(p)],
+            ao.at[side, 0, *part_of(p)],
+            rr.at[side, p],
+        )
+
+    def res_remote(i, p):
+        return remote(res_ends(i, p), rs, sources[i])
+
+    def res_start(i, p):
         def local():
-            pltpu.make_async_copy(*res_ends(i, a)).start()
+            pltpu.make_async_copy(*res_ends(i, p)).start()
 
         def away():
-            res_remote(i, a).start()
+            res_remote(i, p).start()
 
         if i == 0:
             both(itself, local, away)
@@ -817,9 +825,9 @@
         each((2, 3), from_twin, arrive)
         for queries in ((2, 4), (0, 2)):
             attend((6, 8), queries)
-            for a in range(2):
+            for p in range(4):
                 for i in range(queries[1] - 1, queries[0] - 1, -1):
-                    res_start(i, a)
+                    res_start(i, p)
 
     @pl.when(jnp.logical_not(home))
     def _():
@@ -831,22 +839,21 @@
         for piece in range(halves):
             w_row_relay(piece)
 
-    def ao_copy(h, j, a):
-        src = ao.at[h, 2 if j == 3 else 0, a]
-        dst = ao.at[h, j, a]
+    def ao_copy(h, j, p):
+        src = ao.at[h, 2 if j == 3 else 0, *part_of(p)]
+        dst = ao.at[h, j, *part_of(p)]
         dev = across if j == 2 else twin
-        at = 4 * a + (2 + h if j == 2 else j // 2)
+        at = 4 + 4 * h + p if j == 2 else j - 1 + p // 2
         return remote((src, dst, ar.at[at]), as_, dev)
 
-    def own_heads(h, a):
-        ref = ao.at[h, 0, a]
-        pltpu.make_async_copy(ref, ref, rr.at[h, a]).wait()
-        ao_copy(h, 2, a).start()
-        ao_copy(h, 1, a).start()
-
-    def cross_heads(h, a):
-        ao_copy(h, 2, a).wait_recv()
-        ao_copy(h, 3, a).start()
+    def own_heads(h, p):
+        done(ao.at[h, 0, *part_of(p)], rr.at[h, p])
+        ao_copy(h, 2, p).start()
+        ao_copy(h, 1, p).start()
+
+    def cross_heads(h, p):
+        ao_copy(h, 2, p).wait_recv()
+        ao_copy(h, 3, p).start()
 
     step = 2 * HD if cols % (2 * HD) == 0 else cols
     chunks = [slice(c, c + step) for c in range(0, cols, step)]
@@ -858,16 +865,25 @@
 
     heads_ = (side, 1 - side)
     w_rows = [pl.ds(pl.multiple_of(h * HD, HD), HD) for h in heads_]
-    first = jnp.where(home, side, 1 - side)
-    second = 1 - first
+    def in_turn(take, lo, hi):
+        def middle():
+            for at in range(lo, hi):
+                take((side, 1 - side)[at // 4], at % 4)
+
+        def end():
+            for at in range(lo, hi):
+                take((1 - side, side)[at % 2], at // 2)
+
+        both(home, middle, end)
+
 
     def own_plane(a):
-        done(ao.at[:, 1, a], ar.at[4 * a])
+        done(ao.at[:, 1, a], ar.at[a])
         for chunk in chunks:
             acc[a, :, chunk] = project([(0, 0), (0, 1), (1, 0), (1, 1)], a, chunk)
 
     def other_plane(a, result):
-        done(ao.at[:, 3, a], ar.at[4 * a + 1])
+        done(ao.at[:, 3, a], ar.at[2 + a])
         slots = [(0, 2), (0, 3), (1, 2), (1, 3)]
         for chunk in chunks:
             total = acc[a, :, chunk] + project(slots, a, chunk)
@@ -882,9 +898,7 @@
     for i in range(rows // FRAME):
         piece = slice(i * FRAME, (i + 1) * FRAME)
         xbuf[1, piece] = masked(xbuf[1, piece], i)
-    for h in (first, second):
-        for a in range(2):
-            own_heads(h, a)
+    in_turn(own_heads, 0, 8)
     own_plane(0)
     done(wbuf.at[2:4, rest], wxr.at[2 * halves])
     done(wbuf.at[2:4, y_part(1 - y)], wyr)
@@ -901,11 +915,9 @@
     def _():
         done(kv.at[0:2, 0:8], fs)
 
-    cross_heads(first, 0)
+    in_turn(cross_heads, 0, 4)
     own_plane(1)
-    cross_heads(first, 1)
-    cross_heads(second, 0)
-    cross_heads(second, 1)
+    in_turn(cross_heads, 4, 8)
     @pl.when(home)
     def _():
         both(itself, lambda: done(res.at[0:3], rs), lambda: done(res, rs))
@@ -914,6 +926,17 @@
     other_plane(1, d_out)
 
     done(ao.at[:, 1:n_mp], as_)
+
+
+def store(a_ref, b_ref, a_hbm, b_hbm, sems):
+    copies = [
+        pltpu.make_async_copy(a_ref, a_hbm, sems.at[0]),
+        pltpu.make_async_copy(b_ref, b_hbm, sems.at[1]),
+    ]
+    for copy in copies:
+        copy.start()
+    for copy in copies:
+        copy.wait()
 
 
 def gathered_call(n, n_mp, q, dq, k, v, dk, dv, flags, w, gate, x, dx):
@@ -924,7 +947,7 @@
     anywhere = pl.BlockSpec(memory_space=pl.ANY)
     vmem = pl.BlockSpec(memory_space=pltpu.VMEM)
     dma = pltpu.SemaphoreType.DMA
-    return pl.pallas_call(
+    results = pl.pallas_call(
         functools.partial(gathered, n, n_mp),
         out_shape=(pltpu.VMEM(x.shape, BF16), pltpu.VMEM(x.shape, BF16)),
         in_specs=[anywhere] * 11,
@@ -965,14 +988,22 @@
             dma,
             dma,
             dma,
-            dma((heads, 2)),
-            dma,
-            dma((8,)),
+            dma((heads, 4)),
+            dma,
+            dma((12,)),
         ],
         compiler_params=pltpu.CompilerParams(
             collective_id=0, has_side_effects=True, vmem_limit_bytes=65000000
         ),
     )(q, dq, k, v, dk, dv, flags, w, gate, x, dx)
+    whole = jax.ShapeDtypeStruct(x.shape, BF16)
+    return pl.pallas_call(
+        store,
+        out_shape=(whole, whole),
+        in_specs=[vmem, vmem],
+        out_specs=(anywhere, anywhere),
+        scratch_shapes=[dma((2,))],
+    )(*(pltpu.with_memory_space_constraint(r, pltpu.VMEM) for r in results))
 
 
 def gathers(n, n_mp, q, x):

time: 36.3 us -> 35 us (0.964)
  local copies, waits for them, and re-layouts: 1.56 us -> 0 us
    unnamed x2 -> x0, local copies, waits for them, and re-layouts: 1.56 us -> none
    pallas_call x0 -> x1, Pallas kernels: none -> 0.96 us  [gathered_call(): pl.pallas_call(store, out_shape=(whole, whole), in_specs=[vmem, vmem], ou...]
    pallas_call x1, Pallas kernels: 33.7 us -> 33 us  [gathered_call(): pl.pallas_call(functools.partial(gathered, n, n_mp), out_shape=(pltpu.VME...]
where the time goes in v7:
time: 35 us; the launch traced here: 34.6 us
  Pallas kernels  34 us (97%)
  between operations  0.64 us (2%)
    pallas_call x1, Pallas kernels, gathered_call(): pl.pallas_call(functools.partial(gathered, n, n_mp), out_shape=(pltpu.VME...  33 us
    pallas_call x1, Pallas kernels, gathered_call(): pl.pallas_call(store, out_shape=(whole, whole), in_specs=[vmem, vmem], ou...  0.96 us

profile of v7, /device:TPU:0, one launch (start us, length us, event | category | flops | bytes accessed | tf_op | source)
XLA Modules:
  0.0 34.6 jit_solution(14609499754700513932)
XLA Ops:
  0.6 33.0 %shard_map.122 = (bf16[192,1280]{1,0:T(8,128)(2,1)S(1)}, bf16[192,1280]{1,0:T(8,128)(2,1)S(1)}) custom-call(bf16[192,256]{1,0:T(8,128)(2,1)} %q_hbm.1, bf16[192,256]{1,0:T(8,128)(2,1)} %dq_hbm.1, bf16[192,256]{1,0:T(8,128)(2,1)} %k_hbm.1, bf16[192,256]{1,0:T(8,128)(2,1)} %v_hbm.1, bf16[192,256]{1,0:T(8,128)(2,1)} %dk_hbm.1, bf16[192,256]{1,0:T(8,128)(2,1)} %dv_hbm.1, ...), custom_call_target="tpu_custom_call" | custom-call | tf_op jit(solution)/shard_map/pallas_call | solution.py:950
  33.6 1.0 %shard_map.123 = (bf16[192,1280]{1,0:T(8,128)(2,1)}, bf16[192,1280]{1,0:T(8,128)(2,1)}) custom-call(bf16[192,1280]{1,0:T(8,128)(2,1)S(1)} %get-tuple-element.4.a_ref, bf16[192,1280]{1,0:T(8,128)(2,1)S(1)} %get-tuple-element.5.b_ref), custom_call_target="tpu_custom_call" | custom-call | tf_op jit(solution)/shard_map/pallas_call | solution.py:1000

commit v8 on v7

--- a/solution.py
+++ b/solution.py
@@ -771,9 +771,12 @@
             a_s[at] = primal
             g_s[at] = tangent
 
+    cuts = 3 if rows % 48 == 0 else 2
+    parts = 2 * cuts
+
     def part_of(p):
-        half = rows // 2
-        return p // 2, slice(p % 2 * half, (p % 2 + 1) * half)
+        size = rows // cuts
+        return p // cuts, slice(p % cuts * size, (p % cuts + 1) * size)
 
     def res_ends(i, p):
         return (
@@ -825,7 +828,7 @@
         each((2, 3), from_twin, arrive)
         for queries in ((2, 4), (0, 2)):
             attend((6, 8), queries)
-            for p in range(4):
+            for p in range(parts):
                 for i in range(queries[1] - 1, queries[0] - 1, -1):
                     res_start(i, p)
 
@@ -843,7 +846,7 @@
         src = ao.at[h, 2 if j == 3 else 0, *part_of(p)]
         dst = ao.at[h, j, *part_of(p)]
         dev = across if j == 2 else twin
-        at = 4 + 4 * h + p if j == 2 else j - 1 + p // 2
+        at = 4 + parts * h + p if j == 2 else j - 1 + p // cuts
         return remote((src, dst, ar.at[at]), as_, dev)
 
     def own_heads(h, p):
@@ -868,7 +871,7 @@
     def in_turn(take, lo, hi):
         def middle():
             for at in range(lo, hi):
-                take((side, 1 - side)[at // 4], at % 4)
+                take((side, 1 - side)[at // parts], at % parts)
 
         def end():
             for at in range(lo, hi):
@@ -898,7 +901,7 @@
     for i in range(rows // FRAME):
         piece = slice(i * FRAME, (i + 1) * FRAME)
         xbuf[1, piece] = masked(xbuf[1, piece], i)
-    in_turn(own_heads, 0, 8)
+    in_turn(own_heads, 0, 2 * parts)
     own_plane(0)
     done(wbuf.at[2:4, rest], wxr.at[2 * halves])
     done(wbuf.at[2:4, y_part(1 - y)], wyr)
@@ -915,9 +918,9 @@
     def _():
         done(kv.at[0:2, 0:8], fs)
 
-    in_turn(cross_heads, 0, 4)
+    in_turn(cross_heads, 0, parts)
     own_plane(1)
-    in_turn(cross_heads, 4, 8)
+    in_turn(cross_heads, parts, 2 * parts)
     @pl.when(home)
     def _():
         both(itself, lambda: done(res.at[0:3], rs), lambda: done(res, rs))
@@ -929,14 +932,16 @@
 
 
 def store(a_ref, b_ref, a_hbm, b_hbm, sems):
-    copies = [
-        pltpu.make_async_copy(a_ref, a_hbm, sems.at[0]),
-        pltpu.make_async_copy(b_ref, b_hbm, sems.at[1]),
-    ]
+    quarter = a_ref.shape[0] // 4
+    copies = []
+    for i in range(4):
+        part = slice(i * quarter, (i + 1) * quarter)
+        copies.append(pltpu.make_async_copy(a_ref.at[part], a_hbm.at[part], sems.at[0]))
+        copies.append(pltpu.make_async_copy(b_ref.at[part], b_hbm.at[part], sems.at[1]))
     for copy in copies:
         copy.start()
-    for copy in copies:
-        copy.wait()
+    pltpu.make_async_copy(a_ref, a_hbm, sems.at[0]).wait()
+    pltpu.make_async_copy(b_ref, b_hbm, sems.at[1]).wait()
 
 
 def gathered_call(n, n_mp, q, dq, k, v, dk, dv, flags, w, gate, x, dx):
@@ -944,6 +949,7 @@
     cols = x.shape[1]
     heads = width // HD
     halves = 2 if cols % (2 * HD) == 0 else 1
+    cuts = 3 if rows % 48 == 0 else 2
     anywhere = pl.BlockSpec(memory_space=pl.ANY)
     vmem = pl.BlockSpec(memory_space=pltpu.VMEM)
     dma = pltpu.SemaphoreType.DMA
@@ -988,9 +994,9 @@
             dma,
             dma,
             dma,
-            dma((heads, 4)),
-            dma,
-            dma((12,)),
+            dma((heads, 2 * cuts)),
+            dma,
+            dma((4 + 2 * cuts * heads,)),
         ],
         compiler_params=pltpu.CompilerParams(
             collective_id=0, has_side_effects=True, vmem_limit_bytes=65000000
@@ -1008,10 +1014,11 @@
 
 def gathers(n, n_mp, q, x):
     heads = q.shape[1] // HD
+    planes = cores = sides = roles = rows = 2
     return (
-        n_mp == 4
-        and n == 8
-        and heads == 2
+        n_mp == planes * cores
+        and n == sides * roles * rows
+        and heads == sides
         and x.shape[1] % HD == 0
         and q.shape[0] % FRAME == 0
     )

time: 35 us -> 35 us (level)
  no operation moved by 1% of the time
where the time goes in v8:
time: 35 us; the launch traced here: 34.6 us
  Pallas kernels  34 us (97%)
  between operations  0.64 us (2%)
    pallas_call x1, Pallas kernels, gathered_call(): pl.pallas_call(functools.partial(gathered, n, n_mp), out_shape=(pltpu.VME...  33 us
    pallas_call x1, Pallas kernels, gathered_call(): pl.pallas_call(store, out_shape=(whole, whole), in_specs=[vmem, vmem], ou...  0.95 us

profile of v8, /device:TPU:0, one launch (start us, length us, event | category | flops | bytes accessed | tf_op | source)
XLA Modules:
  0.0 34.6 jit_solution(4445078764264601228)
XLA Ops:
  0.6 33.0 %shard_map.122 = (bf16[192,1280]{1,0:T(8,128)(2,1)S(1)}, bf16[192,1280]{1,0:T(8,128)(2,1)S(1)}) custom-call(bf16[192,256]{1,0:T(8,128)(2,1)} %q_hbm.1, bf16[192,256]{1,0:T(8,128)(2,1)} %dq_hbm.1, bf16[192,256]{1,0:T(8,128)(2,1)} %k_hbm.1, bf16[192,256]{1,0:T(8,128)(2,1)} %v_hbm.1, bf16[192,256]{1,0:T(8,128)(2,1)} %dk_hbm.1, bf16[192,256]{1,0:T(8,128)(2,1)} %dv_hbm.1, ...), custom_call_target="tpu_custom_call" | custom-call | tf_op jit(solution)/shard_map/pallas_call | solution.py:956
  33.7 0.9 %shard_map.123 = (bf16[192,1280]{1,0:T(8,128)(2,1)}, bf16[192,1280]{1,0:T(8,128)(2,1)}) custom-call(bf16[192,1280]{1,0:T(8,128)(2,1)S(1)} %get-tuple-element.4.a_ref, bf16[192,1280]{1,0:T(8,128)(2,1)S(1)} %get-tuple-element.5.b_ref), custom_call_target="tpu_custom_call" | custom-call | tf_op jit(solution)/shard_map/pallas_call | solution.py:1006

commit v9 on v8

--- a/solution.py
+++ b/solution.py
@@ -441,6 +441,7 @@
     qr,
     zs,
     kr,
+    kt,
     pr,
     fs,
     wts,
@@ -588,7 +589,7 @@
         crossing = 1 if relayed else (y + core) % 2
         slot = g + 4 * crossing
         src = peer.at[o, pair] if relayed else pack.at[h, pair]
-        return src, kv.at[pair, slot], kr.at[piece - 1, slot]
+        return src, kv.at[pair, slot], kr.at[piece - 1, g]
 
     def home_copy(o, piece):
         return remote(home_ends(o, piece), zs, homes[o])
@@ -703,20 +704,15 @@
 
     def to_twin(pair, g):
         ref = kv.at[2 * pair : 2 * pair + 2, g + mine_at]
-        return remote((ref, ref, kr.at[pair, g + mine_at]), fs, twin)
-
-    def kv_wait(pair, slot):
-        ref = kv.at[2 * pair : 2 * pair + 2, slot]
-        pltpu.make_async_copy(ref, ref, kr.at[pair, slot]).wait()
+        return remote((ref, ref, kt.at[g]), fs, twin)
 
     def arrive(g):
         for pair in range(2):
-            kv_wait(pair, g + mine_at)
+            done(kv.at[2 * pair : 2 * pair + 2, g + mine_at], kr.at[pair, g])
             to_twin(pair, g).start()
 
     def from_twin(g):
-        for pair in range(2):
-            kv_wait(pair, g + twins_at)
+        done(kv.at[:, g + twins_at], kt.at[g])
 
     def q_wait(i):
         pltpu.make_async_copy(qcat.at[i], qcat.at[i], qr.at[i]).wait()
@@ -984,7 +980,8 @@
             dma,
             dma((4,)),
             dma,
-            dma((2, 8)),
+            dma((2, 4)),
+            dma((4,)),
             dma((heads, 3)),
             dma,
             dma,

time: 35 us -> 34.9 us (level)
  no operation moved by 1% of the time
where the time goes in v9:
time: 34.9 us; the launch traced here: 34.6 us
  Pallas kernels  33.9 us (97%)
  between operations  0.64 us (2%)
    pallas_call x1, Pallas kernels, gathered_call(): pl.pallas_call(functools.partial(gathered, n, n_mp), out_shape=(pltpu.VME...  33 us
    pallas_call x1, Pallas kernels, gathered_call(): pl.pallas_call(store, out_shape=(whole, whole), in_specs=[vmem, vmem], ou...  0.95 us

profile of v9, /device:TPU:0, one launch (start us, length us, event | category | flops | bytes accessed | tf_op | source)
XLA Modules:
  0.0 34.6 jit_solution(397274455007578035)
XLA Ops:
  0.6 33.0 %shard_map.122 = (bf16[192,1280]{1,0:T(8,128)(2,1)S(1)}, bf16[192,1280]{1,0:T(8,128)(2,1)S(1)}) custom-call(bf16[192,256]{1,0:T(8,128)(2,1)} %q_hbm.1, bf16[192,256]{1,0:T(8,128)(2,1)} %dq_hbm.1, bf16[192,256]{1,0:T(8,128)(2,1)} %k_hbm.1, bf16[192,256]{1,0:T(8,128)(2,1)} %v_hbm.1, bf16[192,256]{1,0:T(8,128)(2,1)} %dk_hbm.1, bf16[192,256]{1,0:T(8,128)(2,1)} %dv_hbm.1, ...), custom_call_target="tpu_custom_call" | custom-call | tf_op jit(solution)/shard_map/pallas_call | solution.py:952
  33.6 0.9 %shard_map.123 = (bf16[192,1280]{1,0:T(8,128)(2,1)}, bf16[192,1280]{1,0:T(8,128)(2,1)}) custom-call(bf16[192,1280]{1,0:T(8,128)(2,1)S(1)} %get-tuple-element.4.a_ref, bf16[192,1280]{1,0:T(8,128)(2,1)S(1)} %get-tuple-element.5.b_ref), custom_call_target="tpu_custom_call" | custom-call | tf_op jit(solution)/shard_map/pallas_call | solution.py:1003
